TPU v7x, 256 devices: a whole 4x4x8 slice. The times are simulated.
256 devices in a mesh: fsdp: 32 (over z_hi, x, y), ep: 8 (over z_lo, core).
Axes of the slice: x: 4, y: 4, z: 8 (z_hi: 2, z_lo: 4; z = z_hi * 4 + z_lo), core: 2. Of those that a mesh axis runs over, the one named last changes fastest.
Arguments:
- tokens: bfloat16 [32768, 2048], P(('fsdp', 'ep')), may hold values from -24 to 24
- routes: int32 [32768, 6], P(('fsdp', 'ep')), may hold values from 0 to 63, as said below
- route_weight: float32 [32768, 6], P(('fsdp', 'ep')), may hold values from 0.1 to 1
- w_in: bfloat16 [8, 2048, 2, 768], P('ep', 'fsdp'), may hold values from -0.125 to 0.125
- w_down: bfloat16 [8, 768, 2048], P('ep', 'fsdp'), may hold values from -0.21875 to 0.21875
- cotangent: bfloat16 [32768, 2048], P(('fsdp', 'ep')), may hold values from -6 to 6
Outputs:
- layer_out: bfloat16 [32768, 2048], P(('fsdp', 'ep'))
- grad_tokens: bfloat16 [32768, 2048], P(('fsdp', 'ep'))
- grad_in: float32 [8, 2048, 2, 768], P('ep', 'fsdp')
- grad_down: float32 [8, 768, 2048], P('ep', 'fsdp')
Inputs may be any that keep to these rules, and one draw needn't show every extreme that they name: `routes`: each row names 6 different experts. The rows of one device name each window expert 0 to 7 at most 32 times; in every draw every device names some window expert exactly 32 times, and for some index of fsdp one window expert is named exactly 32 times by each device with that index.
All inputs are finite; a program needn't handle non-finite values.
Results may differ from a plain program's by a relative error of at most 0.014.
Values may be sent and summed in bfloat16 or wider, within the bound.
A program may use at most 64 MiB of HBM per device.

v0:
```python
import jax
import jax.numpy as jnp
from jax import lax
from jax.sharding import PartitionSpec as P

D = 2048
FF = 768
CAP = 32


def contract_rows(left, right):
    return lax.dot_general(
        left, right, (((0,), (0,)), ((), ())), preferred_element_type=jnp.float32
    )


def contract_cols(left, right):
    return lax.dot_general(
        left, right, (((1,), (1,)), ((), ())), preferred_element_type=jnp.float32
    )


def local(tokens, routes, route_weight, w_in, w_down, cotangent):
    ep_width = lax.axis_size("ep")
    all_rows = ep_width * CAP
    expert_ids = jnp.arange(ep_width, dtype=jnp.int32)
    route_hits = routes[:, :, None] == expert_ids[None, None, :]
    member = jnp.any(route_hits, axis=1).astype(jnp.int32)
    route_coef = jnp.sum(jnp.where(route_hits, route_weight[:, :, None], 0.0), axis=1)
    slot_rank = jnp.cumsum(member, axis=0) - member
    slot_ids = jnp.arange(CAP, dtype=jnp.int32)
    slot_hits = (slot_rank.T[:, None, :] == slot_ids[None, :, None]) & (member.T[:, None, :] > 0)
    dispatch = slot_hits.astype(jnp.bfloat16)
    slot_coef = jnp.sum(jnp.where(slot_hits, route_coef.T[:, None, :], 0.0), axis=2)
    weighted_dispatch = jnp.where(slot_hits, route_coef.T[:, None, :], 0.0)
    send_x = jnp.einsum("est,td->esd", dispatch, tokens, preferred_element_type=jnp.float32).astype(
        jnp.bfloat16
    )
    dy_rows = jnp.einsum("est,td->esd", dispatch, cotangent, preferred_element_type=jnp.float32)
    send_dy = (dy_rows * slot_coef[:, :, None]).astype(jnp.bfloat16)
    full_in, full_down = (
        lax.all_gather(w_in[0], "fsdp", axis=0, tiled=True),
        lax.all_gather(w_down[0], "fsdp", axis=0, tiled=True),
    )
    flat_in = full_in.reshape(D, 2 * FF)
    recv_x = lax.all_to_all(send_x, "ep", split_axis=0, concat_axis=0, tiled=True)
    rows_x = recv_x.reshape(all_rows, D)
    gate_up = jnp.dot(rows_x, flat_in, preferred_element_type=jnp.float32)
    gate_vals = gate_up[:, :FF]
    up_vals = gate_up[:, FF:]
    sig_gate = jax.nn.sigmoid(gate_vals)
    act_vals = gate_vals * sig_gate
    hidden = (act_vals * up_vals).astype(jnp.bfloat16)
    out_rows = jnp.dot(hidden, full_down, preferred_element_type=jnp.float32).astype(jnp.bfloat16)
    out_rows = out_rows.reshape(ep_width, CAP, D)
    back_out = lax.all_to_all(out_rows, "ep", split_axis=0, concat_axis=0, tiled=True)
    recv_dy = lax.all_to_all(send_dy, "ep", split_axis=0, concat_axis=0, tiled=True)
    rows_dy = recv_dy.reshape(all_rows, D)
    grad_hidden = contract_cols(rows_dy, full_down)
    grad_gate = grad_hidden * up_vals * sig_gate * (1.0 + gate_vals * (1.0 - sig_gate))
    grad_up = grad_hidden * act_vals
    grad_gu = jnp.concatenate([grad_gate, grad_up], axis=1).astype(jnp.bfloat16)
    input_rows = contract_cols(grad_gu, flat_in).astype(jnp.bfloat16).reshape(ep_width, CAP, D)
    term_in = contract_rows(rows_x, grad_gu)
    term_down = contract_rows(hidden, rows_dy)
    grad_in, grad_down = (
        lax.psum_scatter(
            term_in.astype(jnp.bfloat16), "fsdp", scatter_dimension=0, tiled=True
        ).astype(jnp.float32),
        lax.psum_scatter(
            term_down.astype(jnp.bfloat16), "fsdp", scatter_dimension=0, tiled=True
        ).astype(jnp.float32),
    )
    back_dx = lax.all_to_all(input_rows, "ep", split_axis=0, concat_axis=0, tiled=True)
    mixed_sum = jnp.einsum(
        "est,esd->td",
        weighted_dispatch,
        back_out.astype(jnp.float32),
        preferred_element_type=jnp.float32,
    )
    grad_sum = jnp.einsum("est,esd->td", dispatch, back_dx, preferred_element_type=jnp.float32)
    layer_out = mixed_sum.astype(jnp.bfloat16)
    grad_tokens = grad_sum.astype(jnp.bfloat16)
    grad_in = grad_in.reshape(w_in.shape)
    grad_down = grad_down.reshape(w_down.shape)
    return (layer_out, grad_tokens, grad_in, grad_down)


def solution(mesh):
    in_specs = (
        P(("fsdp", "ep"), None),
        P(("fsdp", "ep"), None),
        P(("fsdp", "ep"), None),
        P("ep", "fsdp", None, None),
        P("ep", "fsdp", None),
        P(("fsdp", "ep"), None),
    )
    out_specs = (
        P(("fsdp", "ep"), None),
        P(("fsdp", "ep"), None),
        P("ep", "fsdp", None, None),
        P("ep", "fsdp", None),
    )
    return jax.shard_map(local, mesh=mesh, in_specs=in_specs, out_specs=out_specs, check_vma=False)
```

profile of v0, /device:TPU:2, one launch (start us, length us, event | category | flops | bytes accessed | tf_op | source)
XLA Modules:
  0.0 798.1 jit_solution(17378542734916853659)
XLA Ops:
  9.9 1.5 convolution_convert_fusion.2
  11.3 5.9 all-to-all-start
  17.4 1.5 fusion.4
  18.9 27.7 %all-to-all-done = bf16[8,32,2048]{2,1,0:T(8,128)(2,1)S(1)} async-done(((bf16[8,32,2048]{2,1,0:T(8,128)(2,1)}), bf16[8,32,2048]{2,1,0:T(8,128)(2,1)S(1)}, u32[]{:S(2)}, u32[]{:S(2)}) %all-to-all-start) | async-done | bytes 1048608 | tf_op jit(solution)/shard_map/all_to_all | solution.py:46
  46.6 3.6 all-to-all-start.2
  50.2 109.5 %all-gather.5.cloned.1.call-done = bf16[1,2048,2,768]{3,2,0,1:T(2,128)(2,1)} async-done(((bf16[1,64,2,768]{3,2,0,1:T(2,128)(2,1)}), bf16[1,2048,2,768]{3,2,0,1:T(2,128)(2,1)}) %all-gather.5.cloned.1.call-update) | async-done | bytes 6291472 | tf_op jit(solution)/shard_map/all_gather | solution.py:42
  159.7 4.1 copy.23
  163.8 2.7 copy-done.1
  166.5 2.9 fusion.33
  169.5 88.3 %all-gather.7.cloned.1.call-done = bf16[1,768,2048]{2,1,0:T(8,128)(2,1)} async-done(((bf16[1,24,2048]{2,1,0:T(8,128)(2,1)}), bf16[1,768,2048]{2,1,0:T(8,128)(2,1)}) %all-gather.7.cloned.1.call-update) | async-done | bytes 3145744 | tf_op jit(solution)/shard_map/all_gather | solution.py:43
  257.8 4.3 multiply_convert_fusion.1
  262.1 2.7 convolution_convert_fusion.1
  265.8 4.5 convolution_convert_fusion
  270.3 3.9 fusion.5
  274.1 3.6 all-to-all-start.1
  277.7 5.7 convolution_convert_fusion.3
  283.4 23.6 %all-to-all-done.1 = bf16[8,32,2048]{2,1,0:T(8,128)(2,1)S(1)} async-done(((bf16[8,32,2048]{2,1,0:T(8,128)(2,1)}), bf16[8,32,2048]{2,1,0:T(8,128)(2,1)S(1)}, u32[]{:S(2)}, u32[]{:S(2)}) %all-to-all-start.1) | async-done | bytes 1048608 | tf_op jit(solution)/shard_map/all_to_all | solution.py:56
  306.9 3.6 all-to-all-start.3
  311.6 28.3 %all-to-all-done.3 = bf16[8,32,2048]{2,1,0:T(8,128)(2,1)S(1)} async-done(((bf16[8,32,2048]{2,1,0:T(8,128)(2,1)}), bf16[8,32,2048]{2,1,0:T(8,128)(2,1)S(1)}, u32[]{:S(2)}, u32[]{:S(2)}) %all-to-all-start.3) | async-done | bytes 1048608 | tf_op jit(solution)/shard_map/all_to_all | solution.py:74
  339.9 1.1 fusion.9
  341.1 178.2 %reduce-scatter.5.cloned.1.call-done = bf16[24,2048]{1,0:T(8,128)(2,1)} async-done(((bf16[768,2048]{1,0:T(8,128)(2,1)}), bf16[24,2048]{1,0:T(8,128)(2,1)}) %reduce-scatter.5.cloned.1.call-update) | async-done | bytes 98320 | tf_op jit(solution)/shard_map/reduce_scatter | solution.py:70
  519.2 1.6 bitcast_convert_fusion
  520.8 268.8 %reduce-scatter.3.cloned.1.call-done = bf16[64,1536]{1,0:T(8,128)(2,1)} async-done(((bf16[2048,1536]{1,0:T(8,128)(2,1)}), bf16[64,1536]{1,0:T(8,128)(2,1)}) %reduce-scatter.3.cloned.1.call-update) | async-done | bytes 196624 | tf_op jit(solution)/shard_map/reduce_scatter | solution.py:67
  789.7 1.9 reshape.52
  (30 shorter events, 4.9 us)
Async XLA Ops:
  7.2 2.7 copy-start
  7.2 10.0 %copy-start.4 = (s32[128,6]{0,1:T(8,128)S(1)}, s32[128,6]{0,1:T(8,128)}, u32[]{:S(2)}) copy-start(s32[128,6]{0,1:T(8,128)} %param.7) | copy-start | bytes 9220
  7.2 10.0 %copy-start.5 = (f32[128,6]{0,1:T(8,128)S(1)}, f32[128,6]{0,1:T(8,128)}, u32[]{:S(2)}) copy-start(f32[128,6]{0,1:T(8,128)} %param.8) | copy-start | bytes 9220
  7.2 10.2 %copy-start.2 = (bf16[128,2048]{1,0:T(8,128)(2,1)S(1)}, bf16[128,2048]{1,0:T(8,128)(2,1)}, u32[]{:S(2)}) copy-start(bf16[128,2048]{1,0:T(8,128)(2,1)} %param.11) | copy-start | bytes 1572868
  7.2 152.5 %all-gather.5.cloned.1.call-start = ((), (), s32[]{:S(2)}) async-start(), calls=%async_computation.8 | async-start | bytes 6488064 | tf_op jit(solution)/shard_map/all_gather | solution.py:42
  7.9 249.8 %all-gather.7.cloned.1.call-start = ((), (), s32[]{:S(2)}) async-start(), calls=%async_computation.9 | async-start | bytes 3244032 | tf_op jit(solution)/shard_map/all_gather | solution.py:43
  11.3 35.3 %all-to-all-start = ((bf16[8,32,2048]{2,1,0:T(8,128)(2,1)}), bf16[8,32,2048]{2,1,0:T(8,128)(2,1)S(1)}, u32[]{:S(2)}, u32[]{:S(2)}) async-start(bf16[8,32,2048]{2,1,0:T(8,128)(2,1)} %convolution_convert_fusion.2), calls=%async_computation | async-start | bytes 2097152 | tf_op jit(solution)/shard_map/all_to_all | solution.py:46
  46.6 122.8 %all-to-all-start.2 = ((bf16[8,32,2048]{2,1,0:T(8,128)(2,1)}), bf16[8,32,2048]{2,1,0:T(8,128)(2,1)S(1)}, u32[]{:S(2)}, u32[]{:S(2)}) async-start(bf16[8,32,2048]{2,1,0:T(8,128)(2,1)} %fusion.4), calls=%async_computation.2 | async-start | bytes 2097152 | tf_op jit(solution)/shard_map/all_to_all | solution.py:57
  50.2 469.1 %reduce-scatter.5.cloned.1.call-start = ((), (), s32[]{:S(2)}) async-start(), calls=%async_computation.7 | async-start | bytes 3244032 | tf_op jit(solution)/shard_map/reduce_scatter | solution.py:70
  163.8 2.7 copy-start.1
  264.8 1.0 copy-start.3
  264.8 524.9 %reduce-scatter.3.cloned.1.call-start = ((), (), s32[]{:S(2)}) async-start(), calls=%async_computation.6 | async-start | bytes 6488064 | tf_op jit(solution)/shard_map/reduce_scatter | solution.py:67
  274.1 32.8 %all-to-all-start.1 = ((bf16[8,32,2048]{2,1,0:T(8,128)(2,1)}), bf16[8,32,2048]{2,1,0:T(8,128)(2,1)S(1)}, u32[]{:S(2)}, u32[]{:S(2)}) async-start(bf16[8,32,2048]{2,1,0:T(8,128)(2,1)} %bitcast.7), calls=%async_computation.1 | async-start | bytes 2097152 | tf_op jit(solution)/shard_map/all_to_all | solution.py:56
  306.9 33.0 %all-to-all-start.3 = ((bf16[8,32,2048]{2,1,0:T(8,128)(2,1)}), bf16[8,32,2048]{2,1,0:T(8,128)(2,1)S(1)}, u32[]{:S(2)}, u32[]{:S(2)}) async-start(bf16[8,32,2048]{2,1,0:T(8,128)(2,1)} %bitcast.57), calls=%async_computation.3 | async-start | bytes 2097152 | tf_op jit(solution)/shard_map/all_to_all | solution.py:74
Sparse Core Ops, SparseCore 0:
  11.4 148.2 all-gather.4
  163.1 94.6 all-gather.6
  264.9 254.2 reduce-scatter.4
  525.6 264.0 reduce-scatter.2
where the time goes:
time: 799 us; the launch traced here: 798 us
  waiting for transfers between devices  726 us (91%)
  matrix products  29.2 us (4%)
  starting transfers between devices  16.7 us (2%)
  between operations  13.9 us (2%)
  local copies, waits for them, and re-layouts  9.89 us (1%)
    reduce_scatter x1, waiting for transfers between devices, local(): lax.psum_scatter(term_in.astype(jnp.bfloat16), 'fsdp', scatter_dimension=...  269 us
    reduce_scatter x1, waiting for transfers between devices, local(): lax.psum_scatter(term_down.astype(jnp.bfloat16), 'fsdp', scatter_dimensio...  178 us
    all_gather x1, waiting for transfers between devices, local(): lax.all_gather(w_in[0], 'fsdp', axis=0, tiled=True)  109 us
    all_gather x1, waiting for transfers between devices, local(): lax.all_gather(w_down[0], 'fsdp', axis=0, tiled=True)  88.3 us
    all_to_all x1, waiting for transfers between devices, local(): lax.all_to_all(input_rows, 'ep', split_axis=0, concat_axis=0, tiled=True)  28.3 us
    all_to_all x1, waiting for transfers between devices, local(): lax.all_to_all(send_x, 'ep', split_axis=0, concat_axis=0, tiled=True)  27.7 us
    all_to_all x1, waiting for transfers between devices, local(): lax.all_to_all(out_rows, 'ep', split_axis=0, concat_axis=0, tiled=True)  23.6 us
  transfers between devices with their start and end apart: 8, of which 7 were waited for; matrix products, arithmetic and copies ran while one was open for 4% of the time, Pallas kernels for 0%

commit v1 on v0

v1 whole, which is shorter than its diff:
```python
import jax
import jax.numpy as jnp
from jax import lax
from jax.experimental import pallas as pl
from jax.experimental.pallas import tpu as pltpu
from jax.sharding import PartitionSpec as P

D = 2048
FF = 768
CAP = 32
MESH = pl.DeviceIdType.MESH
F32 = jnp.float32
BF16 = jnp.bfloat16
N_SEM_A = 200
N_SEM_B = 220


def rem(value, modulus):
    return lax.rem(value, jnp.int32(modulus))


def div(value, divisor):
    return lax.div(value, jnp.int32(divisor))


def place():
    f = lax.axis_index("fsdp")
    e = lax.axis_index("ep")
    return rem(div(f, 4), 4), rem(f, 4), div(f, 16) * 4 + div(e, 2), rem(e, 2)


def device(x, y, z, c):
    return (div(z, 4) * 16 + x * 4 + y, rem(z, 4) * 2 + c)


def greet(x, y, z, c):
    barrier = pltpu.get_barrier_semaphore()
    peers = [device(rem(x + o, 4), y, z, c) for o in (1, 3)]
    peers += [device(x, rem(y + o, 4), z, c) for o in (1, 3)]
    peers += [device(x, y, rem(z + 4, 8), c), device(x, y, z, 1 - c)]
    peers += [device(x, y, rem(z + o, 8), k) for o in (1, 7, 2, 6) for k in (0, 1)]
    for peer in peers:
        pl.semaphore_signal(barrier, inc=1, device_id=peer, device_id_type=MESH)
    pl.semaphore_wait(barrier, len(peers))


class Link:
    def __init__(self, send_sem, recv_sem, limit):
        self.send_sem, self.recv_sem, self.limit = send_sem, recv_sem, limit
        self.number, self.sent = {}, []

    def index(self, key):
        number = self.number.setdefault(key, len(self.number))
        assert number < self.limit
        return number

    def send(self, key, src, dst, to):
        k = self.index(key)
        copy = pltpu.make_async_remote_copy(
            src_ref=src, dst_ref=dst, send_sem=self.send_sem.at[k], recv_sem=self.recv_sem.at[k],
            device_id=to, device_id_type=MESH,
        )
        copy.start()
        self.sent.append(copy)

    def wait(self, key, dst):
        k = self.index(key)
        pltpu.make_async_remote_copy(
            src_ref=dst, dst_ref=dst, send_sem=self.send_sem.at[k], recv_sem=self.recv_sem.at[k],
            device_id=place_id(), device_id_type=MESH,
        ).wait_recv()

    def drain(self):
        for copy in self.sent:
            copy.wait_send()


def place_id():
    return (lax.axis_index("fsdp"), lax.axis_index("ep"))


def part(kind, ref, p=None, h=None):
    if p is None:
        return ref
    size = (32 if kind == "in" else 1024) // (1 if h is None else 2)
    start = (32 if kind == "in" else 1024) * p + size * (h or 0)
    if kind == "in":
        return ref.at[pl.ds(start, size), :]
    return ref.at[:, pl.ds(start, size)]


def exchange_targets(x, y, z, c):
    out = []
    for kind, off in ((0, 0), (1, 1), (2, 7), (3, 2 + 4 * c)):
        for k in (0, 1):
            out.append((kind, k, rem(z + off, 8)))
    return out


def gather_kernel(win, wdn, sx, sdy, fin, fdn, rx, rdy, send_sem, recv_sem, a_send, a_recv, local_sem):
    x, y, z, c = place()
    zh = div(z, 4)
    greet(x, y, z, c)
    link = Link(send_sem, recv_sem, N_SEM_A)
    full = {"in": fin, "dn": fdn}
    own = {"in": win, "dn": wdn}
    kinds = ("dn", "in")
    zs = (zh, 1 - zh)
    to_x = {s: device(rem(x + s, 4), y, z, c) for s in (1, 3)}
    to_y = {s: device(x, rem(y + s, 4), z, c) for s in (1, 3)}

    def slot(kind, q, xo, yo, p=None, h=None):
        return part(kind, full[kind].at[zs[q], rem(x + xo, 4), rem(y + yo, 4)], p, h)

    for n, kind in enumerate(kinds):
        link.send(("z", kind), own[kind], slot(kind, 0, 0, 0), device(x, y, rem(z + 4, 8), c))

    def start(q):
        for kind in kinds:
            src = own[kind] if q == 0 else slot(kind, q, 0, 0)
            for s in (1, 3):
                link.send(("x0", q, kind, s), src, slot(kind, q, 0, 0), to_x[s])
                link.send(("y0", q, kind, s), src, slot(kind, q, 0, 0), to_y[s])

    def first(q):
        for kind in kinds:
            for s in (1, 3):
                h = 0 if s == 1 else 1
                link.wait(("x0", q, kind, s), slot(kind, q, 4 - s, 0))
                for p in (0, 1):
                    piece = slot(kind, q, 4 - s, 0, p, h)
                    link.send(("xf", q, kind, p, 0, s), piece, piece, to_x[s])
                for t in (1, 3):
                    piece = slot(kind, q, 4 - s, 0, 0)
                    link.send(("y2", q, kind, 4 - s, t), piece, piece, to_y[t])
                link.wait(("y0", q, kind, s), slot(kind, q, 0, 4 - s))
                for p in (0, 1):
                    piece = slot(kind, q, 0, 4 - s, p, h)
                    link.send(("yf", q, kind, p, 0, s), piece, piece, to_y[s])
                for t in (1, 3):
                    piece = slot(kind, q, 0, 4 - s, 1)
                    link.send(("x2", q, kind, 4 - s, t), piece, piece, to_x[t])

    def second(q):
        for kind in kinds:
            for s in (1, 3):
                h = 0 if s == 1 else 1
                link.wait(("xf", q, kind, 0, 0, s), slot(kind, q, 2, 0, 0, h))
                link.wait(("yf", q, kind, 1, 0, s), slot(kind, q, 0, 2, 1, h))
            for t in (1, 3):
                piece = slot(kind, q, 2, 0, 0)
                link.send(("y2", q, kind, 2, t), piece, piece, to_y[t])
                piece = slot(kind, q, 0, 2, 1)
                link.send(("x2", q, kind, 2, t), piece, piece, to_x[t])

    def third(q, offsets):
        for kind in kinds:
            for o in offsets:
                for s in (1, 3):
                    h = 0 if s == 1 else 1
                    link.wait(("y2", q, kind, o, s), slot(kind, q, o, 4 - s, 0))
                    piece = slot(kind, q, o, 4 - s, 0, h)
                    link.send(("yf", q, kind, 0, o, s), piece, piece, to_y[s])
                    link.wait(("x2", q, kind, o, s), slot(kind, q, 4 - s, o, 1))
                    piece = slot(kind, q, 4 - s, o, 1, h)
                    link.send(("xf", q, kind, 1, o, s), piece, piece, to_x[s])

    def last(q):
        for kind in kinds:
            for s in (1, 3):
                h = 0 if s == 1 else 1
                for o in range(4):
                    link.wait(("yf", q, kind, 0, o, s), slot(kind, q, o, 2, 0, h))
                    link.wait(("xf", q, kind, 1, o, s), slot(kind, q, 2, o, 1, h))

    start(0)
    locals_ = []
    for n, kind in enumerate(kinds):
        locals_.append(pltpu.make_async_copy(own[kind], slot(kind, 0, 0, 0), local_sem.at[n]))
    mine = rem(z, 4) * 2 + c
    locals_.append(pltpu.make_async_copy(sx.at[mine], rx.at[c], local_sem.at[2]))
    locals_.append(pltpu.make_async_copy(sdy.at[mine], rdy.at[c], local_sem.at[3]))
    for copy in locals_:
        copy.start()
    first(0)
    for kind in kinds:
        link.wait(("z", kind), slot(kind, 1, 0, 0))
    start(1)
    rows = []
    for which, (src, dst) in enumerate(((sx, rx), (sdy, rdy))):
        for kind, k, zd in exchange_targets(x, y, z, c):
            if kind == 0:
                if k:
                    continue
                core = 1 - c
            else:
                core = k
            expert = rem(zd, 4) * 2 + core
            number = which * 8 + 2 * kind + c
            copy = pltpu.make_async_remote_copy(
                src_ref=src.at[expert], dst_ref=dst.at[2 * kind + c], send_sem=a_send.at[which * 8 + 2 * kind + k],
                recv_sem=a_recv.at[number], device_id=device(x, y, zd, core), device_id_type=MESH,
            )
            copy.start()
            rows.append(copy)
    second(0)
    third(0, (1, 3))
    first(1)
    third(0, (2,))
    second(1)
    third(1, (1, 3))
    third(1, (2,))
    last(0)
    last(1)
    for which, dst in enumerate((rx, rdy)):
        for number in range(1, 8):
            s = number if number > 1 else 1 - c
            pltpu.make_async_remote_copy(
                src_ref=dst.at[s], dst_ref=dst.at[s], send_sem=a_send.at[which * 8 + number],
                recv_sem=a_recv.at[which * 8 + s], device_id=place_id(), device_id_type=MESH,
            ).wait_recv()
    for copy in locals_:
        copy.wait()
    for copy in rows:
        copy.wait_send()
    link.drain()


def gather(win, wdn, sx, sdy):
    anyspace = pl.BlockSpec(memory_space=pl.ANY)
    return pl.pallas_call(
        gather_kernel,
        name="weights_and_rows_in",
        out_shape=(
            jax.ShapeDtypeStruct((2, 4, 4, 64, 2 * FF), BF16),
            jax.ShapeDtypeStruct((2, 4, 4, 24, D), BF16),
            jax.ShapeDtypeStruct((8, CAP, D), BF16),
            jax.ShapeDtypeStruct((8, CAP, D), BF16),
        ),
        in_specs=[anyspace] * 4,
        out_specs=[anyspace] * 4,
        scratch_shapes=[
            pltpu.SemaphoreType.DMA((N_SEM_A,)),
            pltpu.SemaphoreType.DMA((N_SEM_A,)),
            pltpu.SemaphoreType.DMA((16,)),
            pltpu.SemaphoreType.DMA((16,)),
            pltpu.SemaphoreType.DMA((4,)),
        ],
        compiler_params=pltpu.CompilerParams(collective_id=0, has_side_effects=True),
    )(win, wdn, sx, sdy)


def scatter_kernel(tin_hbm, tdn_hbm, ox, odx, gin, gdn, box, bdx,
                   tin, tdn, a_in, a_dn, b_in, b_dn, c_in, c_dn, d_in, d_dn, e_in, e_dn,
                   send_sem, recv_sem, r_send, r_recv, local_sem):
    x, y, z, c = place()
    zh = div(z, 4)
    e = lax.axis_index("ep")
    link = Link(send_sem, recv_sem, N_SEM_B)
    term = {"in": tin, "dn": tdn}
    buf_a = {"in": a_in, "dn": a_dn}
    buf_b = {"in": b_in, "dn": b_dn}
    buf_c = {"in": c_in, "dn": c_dn}
    buf_d = {"in": d_in, "dn": d_dn}
    buf_e = {"in": e_in, "dn": e_dn}
    kinds = ("dn", "in")
    zs = (1 - zh, zh)
    loads = []
    for q in (0, 1):
        for n, (src, dst) in enumerate(((tdn_hbm, tdn), (tin_hbm, tin))):
            copy = pltpu.make_async_copy(src.at[zs[q]], dst.at[zs[q]], local_sem.at[2 * q + n])
            copy.start()
            loads.append(copy)
    own_rows = []
    for which, (src, dst) in enumerate(((ox, box), (odx, bdx))):
        copy = pltpu.make_async_copy(src.at[c], dst.at[e], local_sem.at[4 + which])
        copy.start()
        own_rows.append(copy)
    greet(x, y, z, c)
    to = {0: {s: device(x, rem(y + s, 4), z, c) for s in (1, 3)},
          1: {s: device(rem(x + s, 4), y, z, c) for s in (1, 3)}}

    def slot(kind, q, p, first, other, h=None):
        xo, yo = (other, first) if p == 0 else (first, other)
        return part(kind, term[kind].at[zs[q], rem(x + xo, 4), rem(y + yo, 4)], p, h)

    def add(dst, *srcs):
        total = dst[...].astype(F32)
        for src in srcs:
            total = total + src[...].astype(F32)
        dst[...] = total.astype(BF16)

    offsets = (2, 1, 3, 0)

    def r1(q):
        for o in offsets:
            for kind in kinds:
                for p in (0, 1):
                    for s, h in ((3, 0), (1, 1)):
                        link.send(("a", q, kind, p, o, s), slot(kind, q, p, 2, o, h),
                                  buf_a[kind].at[p, q, o, h], to[p][s])

    def r2(q):
        for o in offsets:
            for kind in kinds:
                for p in (0, 1):
                    for s, h in ((3, 0), (1, 1)):
                        link.wait(("a", q, kind, p, o, s), buf_a[kind].at[p, q, o, h])
                        add(slot(kind, q, p, s, o, h), buf_a[kind].at[p, q, o, h])
                        link.send(("b", q, kind, p, o, s), slot(kind, q, p, s, o),
                                  buf_b[kind].at[p, q, o, h], to[p][s])

    def r3(q):
        for o in offsets:
            for kind in kinds:
                for p in (0, 1):
                    for s, h in ((3, 0), (1, 1)):
                        link.wait(("b", q, kind, p, o, s), buf_b[kind].at[p, q, o, h])
                    add(slot(kind, q, p, 0, o), buf_b[kind].at[p, q, o, 0], buf_b[kind].at[p, q, o, 1])
                    if o == 2:
                        for s, h in ((3, 0), (1, 1)):
                            link.send(("c", q, kind, p, s), slot(kind, q, p, 0, 2, h),
                                      buf_c[kind].at[p, q, h], to[1 - p][s])
        for s, h in ((3, 0), (1, 1)):
            for kind in kinds:
                for p in (0, 1):
                    link.wait(("c", q, kind, p, s), buf_c[kind].at[p, q, h])
                    add(slot(kind, q, p, 0, s, h), buf_c[kind].at[p, q, h])
                    link.send(("d", q, kind, p, s), slot(kind, q, p, 0, s), buf_d[kind].at[p, q, h], to[1 - p][s])

    def wait_d(q):
        for kind in kinds:
            for p in (0, 1):
                for s, h in ((3, 0), (1, 1)):
                    link.wait(("d", q, kind, p, s), buf_d[kind].at[p, q, h])

    partner = device(x, y, rem(z + 4, 8), c)

    def r4(q):
        wait_d(q)
        for kind in kinds:
            for p in (0, 1):
                add(slot(kind, q, p, 0, 0), buf_d[kind].at[p, q, 0], buf_d[kind].at[p, q, 1])
            link.send(("e", kind), term[kind].at[zs[0], x, y], buf_e[kind], partner)

    loads[0].wait()
    loads[1].wait()
    r1(0)
    rows = []
    for which, (src, dst) in enumerate(((ox, box), (odx, bdx))):
        for number in range(1, 8):
            if number == 1:
                s, zd, core = 1 - c, z, 1 - c
            else:
                off = {2: 7, 3: 7, 4: 1, 5: 1, 6: 6, 7: 2}[number]
                s, zd, core = number, rem(z + off, 8), number % 2
            key = 2 * (number // 2) + c
            copy = pltpu.make_async_remote_copy(
                src_ref=src.at[s], dst_ref=dst.at[e], send_sem=r_send.at[which * 8 + number],
                recv_sem=r_recv.at[which * 8 + key], device_id=device(x, y, zd, core), device_id_type=MESH,
            )
            copy.start()
            rows.append(copy)
    loads[2].wait()
    loads[3].wait()
    r1(1)
    r2(0)
    r2(1)
    r3(0)
    r4(0)
    r3(1)
    wait_d(1)
    for kind in kinds:
        link.wait(("e", kind), buf_e[kind])
    for kind, out in (("dn", gdn), ("in", gin)):
        for p in (0, 1):
            total = slot(kind, 1, p, 0, 0)[...].astype(F32) + buf_d[kind][p, 1, 0].astype(F32)
            total = total + buf_d[kind][p, 1, 1].astype(F32)
            total = total + part(kind, buf_e[kind], p)[...].astype(F32)
            part(kind, out, p)[...] = total
    for which, dst in enumerate((box, bdx)):
        for kind, k, zd in exchange_targets(x, y, z, c):
            if kind == 0:
                if k:
                    continue
                core = 1 - c
            else:
                core = k
            expert = rem(zd, 4) * 2 + core
            number = which * 8 + 2 * kind + core
            pltpu.make_async_remote_copy(
                src_ref=dst.at[expert], dst_ref=dst.at[expert], send_sem=r_send.at[which * 8 + 1],
                recv_sem=r_recv.at[number], device_id=place_id(), device_id_type=MESH,
            ).wait_recv()
    for copy in own_rows:
        copy.wait()
    for copy in rows:
        copy.wait_send()
    link.drain()


def scatter(tin, tdn, out_rows, dx_rows):
    anyspace = pl.BlockSpec(memory_space=pl.ANY)
    vmem = pl.BlockSpec(memory_space=pltpu.VMEM)
    return pl.pallas_call(
        scatter_kernel,
        name="gradients_and_rows_out",
        out_shape=(
            jax.ShapeDtypeStruct((64, 2 * FF), F32),
            jax.ShapeDtypeStruct((24, D), F32),
            jax.ShapeDtypeStruct((8, CAP, D), BF16),
            jax.ShapeDtypeStruct((8, CAP, D), BF16),
        ),
        in_specs=[anyspace] * 4,
        out_specs=[vmem, vmem, anyspace, anyspace],
        scratch_shapes=[
            pltpu.VMEM((2, 4, 4, 64, 2 * FF), BF16),
            pltpu.VMEM((2, 4, 4, 24, D), BF16),
            pltpu.VMEM((2, 2, 4, 2, 16, 2 * FF), BF16),
            pltpu.VMEM((2, 2, 4, 2, 24, 512), BF16),
            pltpu.VMEM((2, 2, 4, 2, 32, 2 * FF), BF16),
            pltpu.VMEM((2, 2, 4, 2, 24, 1024), BF16),
            pltpu.VMEM((2, 2, 2, 16, 2 * FF), BF16),
            pltpu.VMEM((2, 2, 2, 24, 512), BF16),
            pltpu.VMEM((2, 2, 2, 32, 2 * FF), BF16),
            pltpu.VMEM((2, 2, 2, 24, 1024), BF16),
            pltpu.VMEM((64, 2 * FF), BF16),
            pltpu.VMEM((24, D), BF16),
            pltpu.SemaphoreType.DMA((N_SEM_B,)),
            pltpu.SemaphoreType.DMA((N_SEM_B,)),
            pltpu.SemaphoreType.DMA((16,)),
            pltpu.SemaphoreType.DMA((16,)),
            pltpu.SemaphoreType.DMA((6,)),
        ],
        compiler_params=pltpu.CompilerParams(
            collective_id=1, has_side_effects=True, vmem_limit_bytes=48 * 1024 * 1024
        ),
    )(tin, tdn, out_rows, dx_rows)


def contract_rows(left, right):
    return lax.dot_general(left, right, (((0,), (0,)), ((), ())), preferred_element_type=F32)


def contract_cols(left, right):
    return lax.dot_general(left, right, (((1,), (1,)), ((), ())), preferred_element_type=F32)


def local(tokens, routes, route_weight, w_in, w_down, cotangent):
    ep_width = lax.axis_size("ep")
    all_rows = ep_width * CAP
    expert_ids = jnp.arange(ep_width, dtype=jnp.int32)
    route_hits = routes[:, :, None] == expert_ids[None, None, :]
    member = jnp.any(route_hits, axis=1).astype(jnp.int32)
    route_coef = jnp.sum(jnp.where(route_hits, route_weight[:, :, None], 0.0), axis=1)
    slot_rank = jnp.cumsum(member, axis=0) - member
    slot_ids = jnp.arange(CAP, dtype=jnp.int32)
    slot_hits = (slot_rank.T[:, None, :] == slot_ids[None, :, None]) & (member.T[:, None, :] > 0)
    dispatch = slot_hits.astype(BF16)
    slot_coef = jnp.sum(jnp.where(slot_hits, route_coef.T[:, None, :], 0.0), axis=2)
    weighted_dispatch = jnp.where(slot_hits, route_coef.T[:, None, :], 0.0)
    send_x = jnp.einsum("est,td->esd", dispatch, tokens, preferred_element_type=F32).astype(BF16)
    dy_rows = jnp.einsum("est,td->esd", dispatch, cotangent, preferred_element_type=F32)
    send_dy = (dy_rows * slot_coef[:, :, None]).astype(BF16)

    full_in, full_down, recv_x, recv_dy = gather(w_in[0].reshape(64, 2 * FF), w_down[0], send_x, send_dy)
    flat_in = full_in.reshape(D, 2 * FF)
    full_down = full_down.reshape(FF, D)
    rows_x = recv_x.reshape(all_rows, D)
    rows_dy = recv_dy.reshape(all_rows, D)
    gate_up = jnp.dot(rows_x, flat_in, preferred_element_type=F32)
    gate_vals = gate_up[:, :FF]
    up_vals = gate_up[:, FF:]
    sig_gate = jax.nn.sigmoid(gate_vals)
    act_vals = gate_vals * sig_gate
    hidden = (act_vals * up_vals).astype(BF16)
    out_rows = jnp.dot(hidden, full_down, preferred_element_type=F32).astype(BF16)
    grad_hidden = contract_cols(rows_dy, full_down)
    grad_gate = grad_hidden * up_vals * sig_gate * (1.0 + gate_vals * (1.0 - sig_gate))
    grad_up = grad_hidden * act_vals
    grad_gu = jnp.concatenate([grad_gate, grad_up], axis=1).astype(BF16)
    input_rows = contract_cols(grad_gu, flat_in).astype(BF16)
    term_in = contract_rows(rows_x, grad_gu).astype(BF16)
    term_down = contract_rows(hidden, rows_dy).astype(BF16)
    grad_in, grad_down, back_out, back_dx = scatter(
        term_in.reshape(2, 4, 4, 64, 2 * FF), term_down.reshape(2, 4, 4, 24, D),
        out_rows.reshape(ep_width, CAP, D), input_rows.reshape(ep_width, CAP, D),
    )
    mixed_sum = jnp.einsum("est,esd->td", weighted_dispatch, back_out.astype(F32), preferred_element_type=F32)
    grad_sum = jnp.einsum("est,esd->td", dispatch, back_dx, preferred_element_type=F32)
    return (
        mixed_sum.astype(BF16),
        grad_sum.astype(BF16),
        grad_in.reshape(w_in.shape),
        grad_down.reshape(w_down.shape),
    )


def solution(mesh):
    in_specs = (
        P(("fsdp", "ep"), None),
        P(("fsdp", "ep"), None),
        P(("fsdp", "ep"), None),
        P("ep", "fsdp", None, None),
        P("ep", "fsdp", None),
        P(("fsdp", "ep"), None),
    )
    out_specs = (
        P(("fsdp", "ep"), None),
        P(("fsdp", "ep"), None),
        P("ep", "fsdp", None, None),
        P("ep", "fsdp", None),
    )
    return jax.shard_map(local, mesh=mesh, in_specs=in_specs, out_specs=out_specs, check_vma=False)
```

time: 799 us -> 161 us (0.20)
  waiting for transfers between devices: 726 us -> 0 us
  Pallas kernels: 0 us -> 132 us
  starting transfers between devices: 16.7 us -> 0 us
  between operations: 13.9 us -> 0.76 us
    reduce_scatter x2 -> x0, waiting for transfers between devices: 447 us -> none  [the longest x1 269 us: local(): lax.psum_scatter(term_in.astype(jnp.bfloat16), 'fsdp', scatter_dimension=...]
    all_gather x2 -> x0, waiting for transfers between devices: 198 us -> none  [the longest x1 109 us: local(): lax.all_gather(w_in[0], 'fsdp', axis=0, tiled=True)]
    pallas_call x0 -> x2, Pallas kernels: none -> 132 us  [the longest x1 68.4 us: scatter(): pl.pallas_call(scatter_kernel, name='gradients_and_rows_out', out_shape=(...]
    all_to_all x4 -> x0, waiting for transfers between devices: 79.6 us -> none  [the longest x1 28.3 us: local(): lax.all_to_all(input_rows, 'ep', split_axis=0, concat_axis=0, tiled=True)]
    all_to_all x4 -> x0, starting transfers between devices: 16.6 us -> none  [the longest x1 5.9 us: local(): lax.all_to_all(send_x, 'ep', split_axis=0, concat_axis=0, tiled=True)]
  transfers between devices with their start and end apart: 8 -> 0, of which waited for: 7 -> 0; matrix products, arithmetic and copies ran while one was open for 4% -> 0% of each run, Pallas kernels for 0% -> 0%
where the time goes in v1:
time: 161 us
  Pallas kernels  132 us (82%)
  matrix products  22.5 us (14%)
  local copies, waits for them, and re-layouts  4.08 us (3%)
  other arithmetic  1.81 us (1%)
    pallas_call x1, Pallas kernels, scatter(): pl.pallas_call(scatter_kernel, name='gradients_and_rows_out', out_shape=(...  68.4 us
    pallas_call x1, Pallas kernels, gather(): pl.pallas_call(gather_kernel, name='weights_and_rows_in', out_shape=(jax....  63.1 us
    dot_general x2, matrix products, contract_rows(): lax.dot_general(left, right, (((0,), (0,)), ((), ())), preferred_element_...  7.23 us
    dot_general x1, matrix products, local(): gate_up = jnp.dot(rows_x, flat_in, preferred_element_type=F32)  5.03 us

profile of v1, /device:TPU:2, one launch (start us, length us, event | category | flops | bytes accessed | tf_op | source)
XLA Modules:
  0.0 160.7 jit_solution(4367426179103200055)
XLA Ops:
  0.6 0.0 copy-start
  0.6 0.8 fusion.22
  1.4 0.7 select_reduce_fusion.1
  2.1 0.1 copy.14
  2.3 0.1 copy.16
  2.3 0.2 reduce_window_sum.11
  2.6 0.1 select_reduce_fusion
  2.7 1.6 %copy.17 = bf16[8,8,2,768]{3,1,2,0:T(8,128)(2,1)} copy(bf16[8,8,2,768]{3,2,1,0:T(2,128)(2,1)} %bitcast.54) | data formatting | bytes 393216
  4.3 1.4 fusion.sdy
  5.7 2.4 %convolution_convert_fusion.2.sx = bf16[8,32,2048]{2,1,0:T(8,128)(2,1)} fusion(bf16[128,2048]{1,0:T(8,128)(2,1)} %param.6, s32[8,128]{1,0:T(8,128)S(1)} %copy.15, pred[8,128]{1,0:T(8,128)(4,1)S(1)} %copy.16), kind=kOutput, calls=%fused_computation.3 | convolution fusion | flops 134807552 | bytes 1577984 | tf_op jit(solution)/shard_map/est,td->esd/dot_general | solution.py:462
  8.2 63.1 %weights_and_rows_in.1 = (bf16[2,4,4,64,1536]{4,3,2,1,0:T(8,128)(2,1)}, bf16[2,4,4,24,2048]{4,3,2,1,0:T(8,128)(2,1)}, bf16[8,32,2048]{2,1,0:T(8,128)(2,1)}, bf16[8,32,2048]{2,1,0:T(8,128)(2,1)}) custom-call(bf16[64,1536]{1,0:T(8,128)(2,1)} %bitcast.53, bf16[24,2048]{1,0:T(8,128)(2,1)} %bitcast.55, bf16[8,32,2048]{2,1,0:T(8,128)(2,1)} %convolution_convert_fusion.2.sx, ...), custom_call_target="tpu_custom_call" | custom-call | tf_op jit(solution)/shard_map/weights_and_rows_in/pallas_call | solution.py:231
  71.3 0.0 copy-start.2
  71.3 5.0 %fusion.26 = f32[256,1536]{1,0:T(8,128)S(1)} fusion(bf16[256,2048]{1,0:T(8,128)(2,1)} %bitcast.49, bf16[2048,1536]{1,0:T(8,128)(2,1)} %bitcast.58), kind=kOutput, calls=%fused_computation.41 | convolution fusion | flops 1610612736 | bytes 8912896 | tf_op jit(solution)/shard_map/dot_general | solution.py:471
  76.4 1.3 multiply_convert_fusion.2
  77.7 1.0 convolution_convert_fusion.4
  78.7 0.5 copy-done.3
  79.2 1.8 %convolution_convert_fusion.3 = bf16[256,2048]{1,0:T(8,128)(2,1)S(1)} fusion(bf16[2048,1536]{1,0:T(8,128)(2,1)S(1)} %bitcast.59, bf16[256,768]{1,0:T(8,128)(2,1)S(1)} %get-tuple-element.21, bf16[256,768]{1,0:T(8,128)(2,1)S(1)} %get-tuple-element.20), kind=kOutput, calls=%fused_computation.5 | convolution fusion | flops 1612709888 | bytes 8126464 | tf_op jit(solution)/shard_map/dot_general | solution.py:446
  81.0 2.7 %convolution_convert_fusion.1 = bf16[768,2048]{1,0:T(8,128)(2,1)} fusion(bf16[256,768]{1,0:T(8,128)(2,1)S(1)} %get-tuple-element.22, bf16[256,2048]{1,0:T(8,128)(2,1)S(1)} %bitcast.52), kind=kOutput, calls=%fused_computation.1 | convolution fusion | flops 806879232 | bytes 4587520 | tf_op jit(solution)/shard_map/dot_general | solution.py:442
  83.7 4.5 %convolution_convert_fusion = bf16[2048,1536]{1,0:T(8,128)(2,1)} fusion(bf16[256,2048]{1,0:T(8,128)(2,1)S(1)} %bitcast.50, bf16[256,768]{1,0:T(8,128)(2,1)S(1)} %get-tuple-element.21, bf16[256,768]{1,0:T(8,128)(2,1)S(1)} %get-tuple-element.20), kind=kOutput, calls=%fused_computation | convolution fusion | flops 1615331328 | bytes 8126464 | tf_op jit(solution)/shard_map/dot_general | solution.py:442
  88.3 68.4 %gradients_and_rows_out.1 = (f32[64,1536]{1,0:T(8,128)S(1)}, f32[24,2048]{1,0:T(8,128)S(1)}, bf16[8,32,2048]{2,1,0:T(8,128)(2,1)S(1)}, bf16[8,32,2048]{2,1,0:T(8,128)(2,1)S(1)}) custom-call(bf16[2,4,4,64,1536]{4,3,2,1,0:T(8,128)(2,1)} %bitcast.47, bf16[2,4,4,24,2048]{4,3,2,1,0:T(8,128)(2,1)} %bitcast.48, bf16[8,32,2048]{2,1,0:T(8,128)(2,1)S(1)} %bitcast.44, ...), custom_call_target="tpu_custom_call" | custom-call | tf_op jit(solution)/shard_map/gradients_and_rows_out/pallas_call | solution.py:405
  156.7 1.1 fusion.1
  157.8 1.1 fusion.2
  159.0 1.0 reshape.53
  160.0 0.7 copy.19
  (10 shorter events, 0.1 us)
Async XLA Ops:
  0.6 3.7 %copy-start = (bf16[128,2048]{1,0:T(8,128)(2,1)S(1)}, bf16[128,2048]{1,0:T(8,128)(2,1)}, u32[]{:S(2)}) copy-start(bf16[128,2048]{1,0:T(8,128)(2,1)} %param.11) | copy-start | bytes 1572868
  71.3 5.1 %copy-start.2 = (bf16[8,32,2048]{2,1,0:T(8,128)(2,1)S(1)}, bf16[8,32,2048]{2,1,0:T(8,128)(2,1)}, u32[]{:S(2)}) copy-start(bf16[8,32,2048]{2,1,0:T(8,128)(2,1)} %get-tuple-element.13) | copy-start | bytes 3145732
  71.3 5.1 %copy-start.4 = (bf16[2,4,4,24,2048]{4,3,2,1,0:T(8,128)(2,1)S(1)}, bf16[2,4,4,24,2048]{4,3,2,1,0:T(8,128)(2,1)}, u32[]{:S(2)}) copy-start(bf16[2,4,4,24,2048]{4,3,2,1,0:T(8,128)(2,1)} %get-tuple-element.14) | copy-start | bytes 9437188
  76.4 2.8 %copy-start.3 = (bf16[2,4,4,64,1536]{4,3,2,1,0:T(8,128)(2,1)S(1)}, bf16[2,4,4,64,1536]{4,3,2,1,0:T(8,128)(2,1)}, u32[]{:S(2)}) copy-start(bf16[2,4,4,64,1536]{4,3,2,1,0:T(8,128)(2,1)} %get-tuple-element.15) | copy-start | bytes 18874372
  81.0 2.7 %copy-start.1 = (bf16[8,32,2048]{2,1,0:T(8,128)(2,1)S(1)}, bf16[8,32,2048]{2,1,0:T(8,128)(2,1)}, u32[]{:S(2)}) copy-start(bf16[8,32,2048]{2,1,0:T(8,128)(2,1)} %get-tuple-element.12) | copy-start | bytes 3145732

commit v2 on v1

v2 whole, which is shorter than its diff:
```python
import jax
import jax.numpy as jnp
from jax import lax
from jax.experimental import pallas as pl
from jax.experimental.pallas import tpu as pltpu
from jax.sharding import PartitionSpec as P

D = 2048
FF = 768
CAP = 32
MESH = pl.DeviceIdType.MESH
F32 = jnp.float32
BF16 = jnp.bfloat16
N_SEM_A = 200
N_SEM_B = 220
ROWS = 8 * CAP


def rem(value, modulus):
    return lax.rem(value, jnp.int32(modulus))


def div(value, divisor):
    return lax.div(value, jnp.int32(divisor))


def place():
    f = lax.axis_index("fsdp")
    e = lax.axis_index("ep")
    return rem(div(f, 4), 4), rem(f, 4), div(f, 16) * 4 + div(e, 2), rem(e, 2)


def device(x, y, z, c):
    return (div(z, 4) * 16 + x * 4 + y, rem(z, 4) * 2 + c)


def greet(x, y, z, c):
    barrier = pltpu.get_barrier_semaphore()
    peers = [device(rem(x + o, 4), y, z, c) for o in (1, 3)]
    peers += [device(x, rem(y + o, 4), z, c) for o in (1, 3)]
    peers += [device(x, y, rem(z + 4, 8), c), device(x, y, z, 1 - c)]
    peers += [device(x, y, rem(z + o, 8), k) for o in (1, 7, 2, 6) for k in (0, 1)]
    for peer in peers:
        pl.semaphore_signal(barrier, inc=1, device_id=peer, device_id_type=MESH)
    pl.semaphore_wait(barrier, len(peers))


class Link:
    def __init__(self, send_sem, recv_sem, limit):
        self.send_sem, self.recv_sem, self.limit = send_sem, recv_sem, limit
        self.number, self.sent = {}, []

    def index(self, key):
        number = self.number.setdefault(key, len(self.number))
        assert number < self.limit
        return number

    def send(self, key, src, dst, to):
        k = self.index(key)
        copy = pltpu.make_async_remote_copy(
            src_ref=src, dst_ref=dst, send_sem=self.send_sem.at[k], recv_sem=self.recv_sem.at[k],
            device_id=to, device_id_type=MESH,
        )
        copy.start()
        self.sent.append(copy)

    def wait(self, key, dst):
        k = self.index(key)
        pltpu.make_async_remote_copy(
            src_ref=dst, dst_ref=dst, send_sem=self.send_sem.at[k], recv_sem=self.recv_sem.at[k],
            device_id=place_id(), device_id_type=MESH,
        ).wait_recv()

    def drain(self):
        for copy in self.sent:
            copy.wait_send()


def place_id():
    return (lax.axis_index("fsdp"), lax.axis_index("ep"))


def part(kind, ref, p=None, h=None):
    if p is None:
        return ref
    size = (32 if kind == "in" else 1024) // (1 if h is None else 2)
    start = (32 if kind == "in" else 1024) * p + size * (h or 0)
    if kind == "in":
        return ref.at[pl.ds(start, size), :]
    return ref.at[:, pl.ds(start, size)]


def exchange_targets(x, y, z, c):
    out = []
    for kind, off in ((0, 0), (1, 1), (2, 7), (3, 2 + 4 * c)):
        for k in (0, 1):
            out.append((kind, k, rem(z + off, 8)))
    return out


def dot(left, right, dims=((1,), (0,))):
    return lax.dot_general(left, right, (dims, ((), ())), preferred_element_type=F32)


def ds(index, size):
    return pl.ds(pl.multiple_of(index * size, size), size)


def rows_of(ref, cols=None):
    if cols is None:
        return ref[...].reshape(ROWS, D)
    return ref[:, :, cols].reshape(ROWS, cols.size)


def kernel(tok_hbm, cot_hbm, rt, rw, win, wdn, layer, gtok, gin, gdn,
           tok, cot, fin, fdn, wd, sx, sdy, rx, rdy, ox, odx, box, bdx,
           back, whi, wlo, xt, gu, gh, hid, hidt, ggu,
           tin, tdn, a_in, a_dn, b_in, b_dn, c_in, c_dn, d_in, d_dn, e_in, e_dn,
           send_sem, recv_sem, a_send, a_recv, send_sem2, recv_sem2, r_send, r_recv, local_sem):
    x, y, z, c = place()
    zh = div(z, 4)
    e = lax.axis_index("ep")
    greet(x, y, z, c)
    link = Link(send_sem, recv_sem, N_SEM_A)
    full = {"in": fin, "dn": fdn}
    own = {"in": win, "dn": wdn}
    kinds = ("dn", "in")
    zs = (zh, 1 - zh)
    to_x = {s: device(rem(x + s, 4), y, z, c) for s in (1, 3)}
    to_y = {s: device(x, rem(y + s, 4), z, c) for s in (1, 3)}
    partner = device(x, y, rem(z + 4, 8), c)

    def slot(kind, q, xo, yo, p=None, h=None):
        return part(kind, full[kind].at[zs[q], rem(x + xo, 4), rem(y + yo, 4)], p, h)

    def start(q):
        for kind in kinds:
            src = own[kind] if q == 0 else slot(kind, q, 0, 0)
            for s in (1, 3):
                link.send(("x0", q, kind, s), src, slot(kind, q, 0, 0), to_x[s])
                link.send(("y0", q, kind, s), src, slot(kind, q, 0, 0), to_y[s])

    def first(q):
        for kind in kinds:
            for s in (1, 3):
                h = 0 if s == 1 else 1
                link.wait(("x0", q, kind, s), slot(kind, q, 4 - s, 0))
                for p in (0, 1):
                    piece = slot(kind, q, 4 - s, 0, p, h)
                    link.send(("xf", q, kind, p, 0, s), piece, piece, to_x[s])
                for t in (1, 3):
                    piece = slot(kind, q, 4 - s, 0, 0)
                    link.send(("y2", q, kind, 4 - s, t), piece, piece, to_y[t])
                link.wait(("y0", q, kind, s), slot(kind, q, 0, 4 - s))
                for p in (0, 1):
                    piece = slot(kind, q, 0, 4 - s, p, h)
                    link.send(("yf", q, kind, p, 0, s), piece, piece, to_y[s])
                for t in (1, 3):
                    piece = slot(kind, q, 0, 4 - s, 1)
                    link.send(("x2", q, kind, 4 - s, t), piece, piece, to_x[t])

    def second(q):
        for kind in kinds:
            for s in (1, 3):
                h = 0 if s == 1 else 1
                link.wait(("xf", q, kind, 0, 0, s), slot(kind, q, 2, 0, 0, h))
                link.wait(("yf", q, kind, 1, 0, s), slot(kind, q, 0, 2, 1, h))
            for t in (1, 3):
                piece = slot(kind, q, 2, 0, 0)
                link.send(("y2", q, kind, 2, t), piece, piece, to_y[t])
                piece = slot(kind, q, 0, 2, 1)
                link.send(("x2", q, kind, 2, t), piece, piece, to_x[t])

    def third(q, offsets):
        for kind in kinds:
            for o in offsets:
                for s in (1, 3):
                    h = 0 if s == 1 else 1
                    link.wait(("y2", q, kind, o, s), slot(kind, q, o, 4 - s, 0))
                    piece = slot(kind, q, o, 4 - s, 0, h)
                    link.send(("yf", q, kind, 0, o, s), piece, piece, to_y[s])
                    link.wait(("x2", q, kind, o, s), slot(kind, q, 4 - s, o, 1))
                    piece = slot(kind, q, 4 - s, o, 1, h)
                    link.send(("xf", q, kind, 1, o, s), piece, piece, to_x[s])

    def last(q, kind):
        for s in (1, 3):
            h = 0 if s == 1 else 1
            for o in range(4):
                link.wait(("yf", q, kind, 0, o, s), slot(kind, q, o, 2, 0, h))
                link.wait(("xf", q, kind, 1, o, s), slot(kind, q, 2, o, 1, h))

    for kind in kinds:
        link.send(("z", kind), own[kind], slot(kind, 0, 0, 0), partner)
    start(0)
    loads = []
    for n, (src, dst) in enumerate(((tok_hbm, tok), (cot_hbm, cot), (wdn, slot("dn", 0, 0, 0)), (win, slot("in", 0, 0, 0)))):
        copy = pltpu.make_async_copy(src, dst, local_sem.at[n])
        copy.start()
        loads.append(copy)

    experts = lax.broadcasted_iota(jnp.int32, (8, 128), 0)
    member = jnp.zeros((8, 128), F32)
    coef = jnp.zeros((8, 128), F32)
    for k in range(6):
        hit = jnp.broadcast_to(rt[k:k + 1, :], (8, 128)) == experts
        member = member + jnp.where(hit, 1.0, 0.0)
        coef = coef + jnp.where(hit, jnp.broadcast_to(rw[k:k + 1, :], (8, 128)), 0.0)
    before = lax.broadcasted_iota(jnp.int32, (128, 128), 0) < lax.broadcasted_iota(jnp.int32, (128, 128), 1)
    rank = dot(jnp.where(member > 0.5, 1.0, 0.0).astype(BF16), jnp.where(before, 1.0, 0.0).astype(BF16))
    rank = jnp.where(member > 0.5, rank, -1.0)
    ids = lax.broadcasted_iota(jnp.int32, (CAP, 128), 0).astype(F32)
    for copy in loads[:2]:
        copy.wait()
    tok_v, cot_v = tok[...], cot[...]
    for k in range(8):
        hits = jnp.broadcast_to(rank[k:k + 1, :], (CAP, 128)) == ids
        pick = jnp.where(hits, 1.0, 0.0)
        weight = jnp.where(hits, jnp.broadcast_to(coef[k:k + 1, :], (CAP, 128)), 0.0)
        sx[k] = dot(pick.astype(BF16), tok_v).astype(BF16)
        sdy[k] = (dot(pick.astype(BF16), cot_v) * jnp.sum(weight, axis=1, keepdims=True)).astype(BF16)
        high = weight.astype(BF16)
        back[pl.ds(CAP * k, CAP), :] = pick.astype(BF16)
        whi[pl.ds(CAP * k, CAP), :] = high
        wlo[pl.ds(CAP * k, CAP), :] = (weight - high.astype(F32)).astype(BF16)
    mine = rem(z, 4) * 2 + c
    rx[c] = sx[mine]
    rdy[c] = sdy[mine]

    first(0)
    for kind in kinds:
        link.wait(("z", kind), slot(kind, 1, 0, 0))
    start(1)
    rows = []
    for which, (src, dst) in enumerate(((sx, rx), (sdy, rdy))):
        for kind, k, zd in exchange_targets(x, y, z, c):
            if kind == 0:
                if k:
                    continue
                core = 1 - c
            else:
                core = k
            expert = rem(zd, 4) * 2 + core
            copy = pltpu.make_async_remote_copy(
                src_ref=src.at[expert], dst_ref=dst.at[2 * kind + c], send_sem=a_send.at[which * 8 + 2 * kind + k],
                recv_sem=a_recv.at[which * 8 + 2 * kind + c], device_id=device(x, y, zd, core), device_id_type=MESH,
            )
            copy.start()
            rows.append(copy)
    second(0)
    third(0, (1, 3))
    first(1)
    third(0, (2,))
    second(1)
    third(1, (1, 3))
    for which, dst in enumerate((rx, rdy)):
        for number in range(1, 8):
            s = number if number > 1 else 1 - c
            pltpu.make_async_remote_copy(
                src_ref=dst.at[s], dst_ref=dst.at[s], send_sem=a_send.at[which * 8 + number],
                recv_sem=a_recv.at[which * 8 + s], device_id=place_id(), device_id_type=MESH,
            ).wait_recv()
    third(1, (2,))
    for copy in loads[2:]:
        copy.wait()
    last(0, "dn")
    last(0, "in")

    @pl.loop(0, 8)
    def _(n):
        xt[ds(n, 256), :] = rows_of(rx, ds(n, 256)).T

    def gates(q):
        xs = rows_of(rx, ds(zs[q], 1024))

        @pl.loop(0, 6)
        def _(n):
            cols = ds(n, 256)
            value = dot(xs, fin[zs[q], :, :, :, cols].reshape(1024, 256))
            gu[:, cols] = value if q == 0 else gu[:, cols] + value

    gates(0)
    last(1, "dn")

    @pl.loop(0, 8)
    def _(g):
        for n in range(4):
            cols = pl.ds(512 * n, 512)
            wd[ds(g, 96), cols] = fdn[div(g, 4), rem(g, 4), :, :, cols].astype(F32).reshape(96, 512).astype(BF16)

    dy = rows_of(rdy)

    @pl.loop(0, 3)
    def _(n):
        gh[:, ds(n, 256)] = dot(dy, wd[ds(n, 256), :], ((1,), (1,)))

    last(1, "in")
    gates(1)

    @pl.loop(0, 3)
    def _(n):
        cols = ds(n, 256)
        ups = pl.ds(pl.multiple_of(FF + n * 256, 256), 256)
        gate, up, grad = gu[:, cols], gu[:, ups], gh[:, cols]
        sig = jax.nn.sigmoid(gate)
        act = gate * sig
        hidden = (act * up).astype(BF16)
        hid[:, cols] = hidden
        hidt[cols, :] = hidden.T
        ggu[:, cols] = (grad * up * sig * (1.0 + gate * (1.0 - sig))).astype(BF16)
        ggu[:, ups] = (grad * act).astype(BF16)

    zr = (1 - zh, zh)
    link2 = Link(send_sem2, recv_sem2, N_SEM_B)
    term = {"in": tin, "dn": tdn}
    buf_a = {"in": a_in, "dn": a_dn}
    buf_b = {"in": b_in, "dn": b_dn}
    buf_c = {"in": c_in, "dn": c_dn}
    buf_d = {"in": d_in, "dn": d_dn}
    buf_e = {"in": e_in, "dn": e_dn}
    to = {0: to_y, 1: to_x}
    offsets = (2, 1, 3, 0)

    def terms(q, kind):
        if kind == "dn":
            left = hidt[ds(zr[q], 384), :]

            @pl.loop(0, 4)
            def _(n):
                cols = ds(n, 512)
                tdn[zr[q], :, :, :, cols] = dot(left, rows_of(rdy, cols)).reshape(4, 4, 24, 512).astype(BF16)
        else:
            @pl.loop(0, 4)
            def _(i):
                left = xt[ds(zr[q] * 4 + i, 256), :]
                for n in range(3):
                    cols = pl.ds(512 * n, 512)
                    tin[zr[q], i, :, :, cols] = dot(left, ggu[:, cols]).astype(BF16).reshape(4, 64, 512)

    def block(kind, q, p, ring, other, h=None):
        xo, yo = (other, ring) if p == 0 else (ring, other)
        return part(kind, term[kind].at[zr[q], rem(x + xo, 4), rem(y + yo, 4)], p, h)

    def add(dst, *srcs):
        total = dst[...].astype(F32)
        for src in srcs:
            total = total + src[...].astype(F32)
        dst[...] = total.astype(BF16)

    def r1(q, kind):
        for o in offsets:
            for p in (0, 1):
                for s, h in ((3, 0), (1, 1)):
                    link2.send(("a", q, kind, p, o, s), block(kind, q, p, 2, o, h),
                               buf_a[kind].at[p, q, o, h], to[p][s])

    def r2(q):
        for kind in kinds:
            for o in offsets:
                for p in (0, 1):
                    for s, h in ((3, 0), (1, 1)):
                        link2.wait(("a", q, kind, p, o, s), buf_a[kind].at[p, q, o, h])
                        add(block(kind, q, p, s, o, h), buf_a[kind].at[p, q, o, h])
                        link2.send(("b", q, kind, p, o, s), block(kind, q, p, s, o),
                                   buf_b[kind].at[p, q, o, h], to[p][s])

    def r3(q):
        for kind in kinds:
            for o in offsets:
                for p in (0, 1):
                    for s, h in ((3, 0), (1, 1)):
                        link2.wait(("b", q, kind, p, o, s), buf_b[kind].at[p, q, o, h])
                    add(block(kind, q, p, 0, o), buf_b[kind].at[p, q, o, 0], buf_b[kind].at[p, q, o, 1])
                    if o == 2:
                        for s, h in ((3, 0), (1, 1)):
                            link2.send(("c", q, kind, p, s), block(kind, q, p, 0, 2, h),
                                       buf_c[kind].at[p, q, h], to[1 - p][s])
            for s, h in ((3, 0), (1, 1)):
                for p in (0, 1):
                    link2.wait(("c", q, kind, p, s), buf_c[kind].at[p, q, h])
                    add(block(kind, q, p, 0, s, h), buf_c[kind].at[p, q, h])
                    link2.send(("d", q, kind, p, s), block(kind, q, p, 0, s), buf_d[kind].at[p, q, h], to[1 - p][s])

    def wait_d(q, kind):
        for p in (0, 1):
            for s, h in ((3, 0), (1, 1)):
                link2.wait(("d", q, kind, p, s), buf_d[kind].at[p, q, h])

    def r4(q):
        for kind in kinds:
            wait_d(q, kind)
            for p in (0, 1):
                add(block(kind, q, p, 0, 0), buf_d[kind].at[p, q, 0], buf_d[kind].at[p, q, 1])
            link2.send(("e", kind), term[kind].at[zr[0], x, y], buf_e[kind], partner)

    for q in (0, 1):
        for kind in kinds:
            terms(q, kind)
            r1(q, kind)

    def rows_back(which, src, dst):
        for number in range(1, 8):
            if number == 1:
                s, zd, core = 1 - c, z, 1 - c
            else:
                off = {2: 7, 3: 7, 4: 1, 5: 1, 6: 6, 7: 2}[number]
                s, zd, core = number, rem(z + off, 8), number % 2
            copy = pltpu.make_async_remote_copy(
                src_ref=src.at[s], dst_ref=dst.at[e], send_sem=r_send.at[which * 8 + number],
                recv_sem=r_recv.at[which * 8 + 2 * (number // 2) + c], device_id=device(x, y, zd, core),
                device_id_type=MESH,
            )
            copy.start()
            rows.append(copy)
        dst[e] = src[c]

    hidden = hid[...]

    @pl.loop(0, 8)
    def _(n):
        cols = ds(n, 256)
        ox[:, :, cols] = dot(hidden, wd[:, cols]).astype(BF16).reshape(8, CAP, 256)

    rows_back(0, ox, box)
    gated = ggu[...]

    @pl.loop(0, 8)
    def _(g):
        value = dot(gated, fin[div(g, 4), rem(g, 4)].reshape(256, 2 * FF), ((1,), (1,)))
        odx[:, :, ds(g, 256)] = value.astype(BF16).reshape(8, CAP, 256)

    rows_back(1, odx, bdx)
    r2(0)
    r2(1)
    r3(0)
    r4(0)
    for which, dst in enumerate((box, bdx)):
        for kind, k, zd in exchange_targets(x, y, z, c):
            if kind == 0:
                if k:
                    continue
                core = 1 - c
            else:
                core = k
            expert = rem(zd, 4) * 2 + core
            pltpu.make_async_remote_copy(
                src_ref=dst.at[expert], dst_ref=dst.at[expert], send_sem=r_send.at[which * 8 + 1],
                recv_sem=r_recv.at[which * 8 + 2 * kind + core], device_id=place_id(), device_id_type=MESH,
            ).wait_recv()
    back_t, high_t, low_t = back[...].T, whi[...].T, wlo[...].T

    @pl.loop(0, 4)
    def _(n):
        cols = ds(n, 512)
        value = rows_of(box, cols)
        layer[:, cols] = (dot(high_t, value) + dot(low_t, value)).astype(BF16)
        gtok[:, cols] = dot(back_t, rows_of(bdx, cols)).astype(BF16)

    r3(1)
    for kind, out in (("dn", gdn), ("in", gin)):
        wait_d(1, kind)
        link2.wait(("e", kind), buf_e[kind])
        for p in (0, 1):
            total = block(kind, 1, p, 0, 0)[...].astype(F32) + buf_d[kind][p, 1, 0].astype(F32)
            total = total + buf_d[kind][p, 1, 1].astype(F32)
            total = total + part(kind, buf_e[kind], p)[...].astype(F32)
            part(kind, out, p)[...] = total
    for copy in rows:
        copy.wait_send()
    link.drain()
    link2.drain()


def call(tokens, cotangent, routes, weights, win, wdn):
    anyspace = pl.BlockSpec(memory_space=pl.ANY)
    vmem = pl.BlockSpec(memory_space=pltpu.VMEM)
    rows = pltpu.VMEM((8, CAP, D), BF16)
    return pl.pallas_call(
        kernel,
        name="expert_window",
        out_shape=(
            jax.ShapeDtypeStruct((128, D), BF16),
            jax.ShapeDtypeStruct((128, D), BF16),
            jax.ShapeDtypeStruct((64, 2 * FF), F32),
            jax.ShapeDtypeStruct((24, D), F32),
        ),
        in_specs=[anyspace, anyspace, vmem, vmem, anyspace, anyspace],
        out_specs=[vmem] * 4,
        scratch_shapes=[
            pltpu.VMEM((128, D), BF16),
            pltpu.VMEM((128, D), BF16),
            pltpu.VMEM((2, 4, 4, 64, 2 * FF), BF16),
            pltpu.VMEM((2, 4, 4, 24, D), BF16),
            pltpu.VMEM((FF, D), BF16),
            rows, rows, rows, rows, rows, rows, rows, rows,
            pltpu.VMEM((ROWS, 128), BF16),
            pltpu.VMEM((ROWS, 128), BF16),
            pltpu.VMEM((ROWS, 128), BF16),
            pltpu.VMEM((D, ROWS), BF16),
            pltpu.VMEM((ROWS, 2 * FF), F32),
            pltpu.VMEM((ROWS, FF), F32),
            pltpu.VMEM((ROWS, FF), BF16),
            pltpu.VMEM((FF, ROWS), BF16),
            pltpu.VMEM((ROWS, 2 * FF), BF16),
            pltpu.VMEM((2, 4, 4, 64, 2 * FF), BF16),
            pltpu.VMEM((2, 4, 4, 24, D), BF16),
            pltpu.VMEM((2, 2, 4, 2, 16, 2 * FF), BF16),
            pltpu.VMEM((2, 2, 4, 2, 24, 512), BF16),
            pltpu.VMEM((2, 2, 4, 2, 32, 2 * FF), BF16),
            pltpu.VMEM((2, 2, 4, 2, 24, 1024), BF16),
            pltpu.VMEM((2, 2, 2, 16, 2 * FF), BF16),
            pltpu.VMEM((2, 2, 2, 24, 512), BF16),
            pltpu.VMEM((2, 2, 2, 32, 2 * FF), BF16),
            pltpu.VMEM((2, 2, 2, 24, 1024), BF16),
            pltpu.VMEM((64, 2 * FF), BF16),
            pltpu.VMEM((24, D), BF16),
            pltpu.SemaphoreType.DMA((N_SEM_A,)),
            pltpu.SemaphoreType.DMA((N_SEM_A,)),
            pltpu.SemaphoreType.DMA((16,)),
            pltpu.SemaphoreType.DMA((16,)),
            pltpu.SemaphoreType.DMA((N_SEM_B,)),
            pltpu.SemaphoreType.DMA((N_SEM_B,)),
            pltpu.SemaphoreType.DMA((16,)),
            pltpu.SemaphoreType.DMA((16,)),
            pltpu.SemaphoreType.DMA((4,)),
        ],
        compiler_params=pltpu.CompilerParams(
            collective_id=0, has_side_effects=True, vmem_limit_bytes=60 * 1024 * 1024
        ),
    )(tokens, cotangent, routes, weights, win, wdn)


def local(tokens, routes, route_weight, w_in, w_down, cotangent):
    layer_out, grad_tokens, grad_in, grad_down = call(
        tokens, cotangent, routes.T, route_weight.T, w_in[0].reshape(64, 2 * FF), w_down[0]
    )
    return layer_out, grad_tokens, grad_in.reshape(w_in.shape), grad_down.reshape(w_down.shape)


def solution(mesh):
    in_specs = (
        P(("fsdp", "ep"), None),
        P(("fsdp", "ep"), None),
        P(("fsdp", "ep"), None),
        P("ep", "fsdp", None, None),
        P("ep", "fsdp", None),
        P(("fsdp", "ep"), None),
    )
    out_specs = (
        P(("fsdp", "ep"), None),
        P(("fsdp", "ep"), None),
        P("ep", "fsdp", None, None),
        P("ep", "fsdp", None),
    )
    return jax.shard_map(local, mesh=mesh, in_specs=in_specs, out_specs=out_specs, check_vma=False)
```

time: 161 us -> 145 us (0.901)
  matrix products: 22.5 us -> 0 us
  Pallas kernels: 132 us -> 137 us
  local copies, waits for them, and re-layouts: 4.08 us -> 6.71 us
  other arithmetic: 1.81 us -> 0 us
    dot_general x10 -> x0, matrix products: 22.5 us -> none  [the longest x2 7.23 us: contract_rows(): lax.dot_general(left, right, (((0,), (0,)), ((), ())), preferred_element_...]
    pallas_call x2 -> x1, Pallas kernels: 132 us -> 137 us  [call(): pl.pallas_call(kernel, name='expert_window', out_shape=(jax.ShapeDtypeStr...]
    unnamed x12 -> x10, local copies, waits for them, and re-layouts: 2.84 us -> 4.65 us
where the time goes in v2:
time: 145 us
  Pallas kernels  137 us (94%)
  local copies, waits for them, and re-layouts  6.71 us (5%)
    pallas_call x1, Pallas kernels, call(): pl.pallas_call(kernel, name='expert_window', out_shape=(jax.ShapeDtypeStr...  137 us
    unnamed x10, local copies, waits for them, and re-layouts  4.65 us

profile of v2, /device:TPU:2, one launch (start us, length us, event | category | flops | bytes accessed | tf_op | source)
XLA Modules:
  0.0 144.5 jit_solution(7770162289408486601)
XLA Ops:
  0.6 1.6 %copy.10 = bf16[8,8,2,768]{3,1,2,0:T(8,128)(2,1)} copy(bf16[8,8,2,768]{3,2,1,0:T(2,128)(2,1)} %bitcast.8) | data formatting | bytes 393216
  2.3 137.2 %expert_window.1 = (bf16[128,2048]{1,0:T(8,128)(2,1)}, bf16[128,2048]{1,0:T(8,128)(2,1)}, f32[64,1536]{1,0:T(8,128)}, f32[24,2048]{1,0:T(8,128)}) custom-call(bf16[128,2048]{1,0:T(8,128)(2,1)} %tok_hbm.1, bf16[128,2048]{1,0:T(8,128)(2,1)} %cot_hbm.1, s32[6,128]{1,0:T(8,128)} %bitcast.11, f32[6,128]{1,0:T(8,128)} %bitcast.12, bf16[64,1536]{1,0:T(8,128)(2,1)} %bitcast.7, ...), custom_call_target="tpu_custom_call" | custom-call | tf_op jit(solution)/shard_map/expert_window/pallas_call | solution.py:478
  139.5 0.0 copy-start.1
  139.5 2.1 %reshape.14 = f32[1,64,2,768]{3,2,1,0:T(2,128)} reshape(f32[64,1536]{1,0:T(8,128)} %get-tuple-element.10) | data formatting | bytes 786432 | tf_op jit(solution)/shard_map/reshape | solution.py:537
  141.5 0.0 copy-done.1
  141.5 0.0 copy-start
  141.5 0.8 copy.14
  142.3 0.4 copy-done
  142.8 0.0 copy-start.2
  142.8 0.8 copy.15
  143.6 0.3 copy-done.2
  143.9 0.7 copy.16
Async XLA Ops:
  139.5 2.1 %copy-start.1 = (bf16[128,2048]{1,0:T(8,128)(2,1)S(1)}, bf16[128,2048]{1,0:T(8,128)(2,1)}, u32[]{:S(2)}) copy-start(bf16[128,2048]{1,0:T(8,128)(2,1)} %get-tuple-element.16) | copy-start | bytes 1572868
  141.5 1.2 copy-start
  142.8 1.1 copy-start.2

commit v3 on v2

--- a/solution.py
+++ b/solution.py
@@ -124,7 +124,6 @@
     link = Link(send_sem, recv_sem, N_SEM_A)
     full = {"in": fin, "dn": fdn}
     own = {"in": win, "dn": wdn}
-    kinds = ("dn", "in")
     zs = (zh, 1 - zh)
     to_x = {s: device(rem(x + s, 4), y, z, c) for s in (1, 3)}
     to_y = {s: device(x, rem(y + s, 4), z, c) for s in (1, 3)}
@@ -133,55 +132,51 @@
     def slot(kind, q, xo, yo, p=None, h=None):
         return part(kind, full[kind].at[zs[q], rem(x + xo, 4), rem(y + yo, 4)], p, h)
 
-    def start(q):
-        for kind in kinds:
-            src = own[kind] if q == 0 else slot(kind, q, 0, 0)
-            for s in (1, 3):
-                link.send(("x0", q, kind, s), src, slot(kind, q, 0, 0), to_x[s])
-                link.send(("y0", q, kind, s), src, slot(kind, q, 0, 0), to_y[s])
-
-    def first(q):
-        for kind in kinds:
+    def start(q, kind):
+        src = own[kind] if q == 0 else slot(kind, q, 0, 0)
+        for s in (1, 3):
+            link.send(("x0", q, kind, s), src, slot(kind, q, 0, 0), to_x[s])
+            link.send(("y0", q, kind, s), src, slot(kind, q, 0, 0), to_y[s])
+
+    def first(q, kind):
+        for s in (1, 3):
+            h = 0 if s == 1 else 1
+            link.wait(("x0", q, kind, s), slot(kind, q, 4 - s, 0))
+            for p in (0, 1):
+                piece = slot(kind, q, 4 - s, 0, p, h)
+                link.send(("xf", q, kind, p, 0, s), piece, piece, to_x[s])
+            for t in (1, 3):
+                piece = slot(kind, q, 4 - s, 0, 0)
+                link.send(("y2", q, kind, 4 - s, t), piece, piece, to_y[t])
+            link.wait(("y0", q, kind, s), slot(kind, q, 0, 4 - s))
+            for p in (0, 1):
+                piece = slot(kind, q, 0, 4 - s, p, h)
+                link.send(("yf", q, kind, p, 0, s), piece, piece, to_y[s])
+            for t in (1, 3):
+                piece = slot(kind, q, 0, 4 - s, 1)
+                link.send(("x2", q, kind, 4 - s, t), piece, piece, to_x[t])
+
+    def second(q, kind):
+        for s in (1, 3):
+            h = 0 if s == 1 else 1
+            link.wait(("xf", q, kind, 0, 0, s), slot(kind, q, 2, 0, 0, h))
+            link.wait(("yf", q, kind, 1, 0, s), slot(kind, q, 0, 2, 1, h))
+        for t in (1, 3):
+            piece = slot(kind, q, 2, 0, 0)
+            link.send(("y2", q, kind, 2, t), piece, piece, to_y[t])
+            piece = slot(kind, q, 0, 2, 1)
+            link.send(("x2", q, kind, 2, t), piece, piece, to_x[t])
+
+    def third(q, kind, offsets):
+        for o in offsets:
             for s in (1, 3):
                 h = 0 if s == 1 else 1
-                link.wait(("x0", q, kind, s), slot(kind, q, 4 - s, 0))
-                for p in (0, 1):
-                    piece = slot(kind, q, 4 - s, 0, p, h)
-                    link.send(("xf", q, kind, p, 0, s), piece, piece, to_x[s])
-                for t in (1, 3):
-                    piece = slot(kind, q, 4 - s, 0, 0)
-                    link.send(("y2", q, kind, 4 - s, t), piece, piece, to_y[t])
-                link.wait(("y0", q, kind, s), slot(kind, q, 0, 4 - s))
-                for p in (0, 1):
-                    piece = slot(kind, q, 0, 4 - s, p, h)
-                    link.send(("yf", q, kind, p, 0, s), piece, piece, to_y[s])
-                for t in (1, 3):
-                    piece = slot(kind, q, 0, 4 - s, 1)
-                    link.send(("x2", q, kind, 4 - s, t), piece, piece, to_x[t])
-
-    def second(q):
-        for kind in kinds:
-            for s in (1, 3):
-                h = 0 if s == 1 else 1
-                link.wait(("xf", q, kind, 0, 0, s), slot(kind, q, 2, 0, 0, h))
-                link.wait(("yf", q, kind, 1, 0, s), slot(kind, q, 0, 2, 1, h))
-            for t in (1, 3):
-                piece = slot(kind, q, 2, 0, 0)
-                link.send(("y2", q, kind, 2, t), piece, piece, to_y[t])
-                piece = slot(kind, q, 0, 2, 1)
-                link.send(("x2", q, kind, 2, t), piece, piece, to_x[t])
-
-    def third(q, offsets):
-        for kind in kinds:
-            for o in offsets:
-                for s in (1, 3):
-                    h = 0 if s == 1 else 1
-                    link.wait(("y2", q, kind, o, s), slot(kind, q, o, 4 - s, 0))
-                    piece = slot(kind, q, o, 4 - s, 0, h)
-                    link.send(("yf", q, kind, 0, o, s), piece, piece, to_y[s])
-                    link.wait(("x2", q, kind, o, s), slot(kind, q, 4 - s, o, 1))
-                    piece = slot(kind, q, 4 - s, o, 1, h)
-                    link.send(("xf", q, kind, 1, o, s), piece, piece, to_x[s])
+                link.wait(("y2", q, kind, o, s), slot(kind, q, o, 4 - s, 0))
+                piece = slot(kind, q, o, 4 - s, 0, h)
+                link.send(("yf", q, kind, 0, o, s), piece, piece, to_y[s])
+                link.wait(("x2", q, kind, o, s), slot(kind, q, 4 - s, o, 1))
+                piece = slot(kind, q, 4 - s, o, 1, h)
+                link.send(("xf", q, kind, 1, o, s), piece, piece, to_x[s])
 
     def last(q, kind):
         for s in (1, 3):
@@ -190,9 +185,9 @@
                 link.wait(("yf", q, kind, 0, o, s), slot(kind, q, o, 2, 0, h))
                 link.wait(("xf", q, kind, 1, o, s), slot(kind, q, 2, o, 1, h))
 
-    for kind in kinds:
+    for kind in ("in", "dn"):
         link.send(("z", kind), own[kind], slot(kind, 0, 0, 0), partner)
-    start(0)
+    start(0, "in")
     loads = []
     for n, (src, dst) in enumerate(((tok_hbm, tok), (cot_hbm, cot), (wdn, slot("dn", 0, 0, 0)), (win, slot("in", 0, 0, 0)))):
         copy = pltpu.make_async_copy(src, dst, local_sem.at[n])
@@ -227,10 +222,10 @@
     rx[c] = sx[mine]
     rdy[c] = sdy[mine]
 
-    first(0)
-    for kind in kinds:
-        link.wait(("z", kind), slot(kind, 1, 0, 0))
-    start(1)
+    first(0, "in")
+    second(0, "in")
+    link.wait(("z", "in"), slot("in", 1, 0, 0))
+    start(1, "in")
     rows = []
     for which, (src, dst) in enumerate(((sx, rx), (sdy, rdy))):
         for kind, k, zd in exchange_targets(x, y, z, c):
@@ -247,28 +242,27 @@
             )
             copy.start()
             rows.append(copy)
-    second(0)
-    third(0, (1, 3))
-    first(1)
-    third(0, (2,))
-    second(1)
-    third(1, (1, 3))
-    for which, dst in enumerate((rx, rdy)):
+    third(0, "in", (1, 3))
+    start(0, "dn")
+    first(1, "in")
+    third(0, "in", (2,))
+    link.wait(("z", "dn"), slot("dn", 1, 0, 0))
+    start(1, "dn")
+    second(1, "in")
+    first(0, "dn")
+    third(1, "in", (1, 3))
+    first(1, "dn")
+    second(0, "dn")
+    third(1, "in", (2,))
+    second(1, "dn")
+
+    def rows_here(which, dst):
         for number in range(1, 8):
             s = number if number > 1 else 1 - c
             pltpu.make_async_remote_copy(
                 src_ref=dst.at[s], dst_ref=dst.at[s], send_sem=a_send.at[which * 8 + number],
                 recv_sem=a_recv.at[which * 8 + s], device_id=place_id(), device_id_type=MESH,
             ).wait_recv()
-    third(1, (2,))
-    for copy in loads[2:]:
-        copy.wait()
-    last(0, "dn")
-    last(0, "in")
-
-    @pl.loop(0, 8)
-    def _(n):
-        xt[ds(n, 256), :] = rows_of(rx, ds(n, 256)).T
 
     def gates(q):
         xs = rows_of(rx, ds(zs[q], 1024))
@@ -279,36 +273,28 @@
             value = dot(xs, fin[zs[q], :, :, :, cols].reshape(1024, 256))
             gu[:, cols] = value if q == 0 else gu[:, cols] + value
 
+    for copy in loads[2:]:
+        copy.wait()
+    rows_here(0, rx)
+    last(0, "in")
     gates(0)
-    last(1, "dn")
-
-    @pl.loop(0, 8)
-    def _(g):
-        for n in range(4):
-            cols = pl.ds(512 * n, 512)
-            wd[ds(g, 96), cols] = fdn[div(g, 4), rem(g, 4), :, :, cols].astype(F32).reshape(96, 512).astype(BF16)
-
-    dy = rows_of(rdy)
-
-    @pl.loop(0, 3)
-    def _(n):
-        gh[:, ds(n, 256)] = dot(dy, wd[ds(n, 256), :], ((1,), (1,)))
-
+    third(0, "dn", (1, 3))
+    third(1, "dn", (1, 3))
     last(1, "in")
     gates(1)
+    third(0, "dn", (2,))
+    third(1, "dn", (2,))
 
     @pl.loop(0, 3)
     def _(n):
         cols = ds(n, 256)
         ups = pl.ds(pl.multiple_of(FF + n * 256, 256), 256)
-        gate, up, grad = gu[:, cols], gu[:, ups], gh[:, cols]
-        sig = jax.nn.sigmoid(gate)
-        act = gate * sig
-        hidden = (act * up).astype(BF16)
+        gate = gu[:, cols]
+        hidden = (gate * jax.nn.sigmoid(gate) * gu[:, ups]).astype(BF16)
         hid[:, cols] = hidden
         hidt[cols, :] = hidden.T
-        ggu[:, cols] = (grad * up * sig * (1.0 + gate * (1.0 - sig))).astype(BF16)
-        ggu[:, ups] = (grad * act).astype(BF16)
+
+    rows_here(1, rdy)
 
     zr = (1 - zh, zh)
     link2 = Link(send_sem2, recv_sem2, N_SEM_B)
@@ -354,49 +340,80 @@
                     link2.send(("a", q, kind, p, o, s), block(kind, q, p, 2, o, h),
                                buf_a[kind].at[p, q, o, h], to[p][s])
 
-    def r2(q):
-        for kind in kinds:
-            for o in offsets:
-                for p in (0, 1):
+    def r2(q, kind):
+        for o in offsets:
+            for p in (0, 1):
+                for s, h in ((3, 0), (1, 1)):
+                    link2.wait(("a", q, kind, p, o, s), buf_a[kind].at[p, q, o, h])
+                    add(block(kind, q, p, s, o, h), buf_a[kind].at[p, q, o, h])
+                    link2.send(("b", q, kind, p, o, s), block(kind, q, p, s, o),
+                               buf_b[kind].at[p, q, o, h], to[p][s])
+
+    def r3(q, kind):
+        for o in offsets:
+            for p in (0, 1):
+                for s, h in ((3, 0), (1, 1)):
+                    link2.wait(("b", q, kind, p, o, s), buf_b[kind].at[p, q, o, h])
+                add(block(kind, q, p, 0, o), buf_b[kind].at[p, q, o, 0], buf_b[kind].at[p, q, o, 1])
+                if o == 2:
                     for s, h in ((3, 0), (1, 1)):
-                        link2.wait(("a", q, kind, p, o, s), buf_a[kind].at[p, q, o, h])
-                        add(block(kind, q, p, s, o, h), buf_a[kind].at[p, q, o, h])
-                        link2.send(("b", q, kind, p, o, s), block(kind, q, p, s, o),
-                                   buf_b[kind].at[p, q, o, h], to[p][s])
-
-    def r3(q):
-        for kind in kinds:
-            for o in offsets:
-                for p in (0, 1):
-                    for s, h in ((3, 0), (1, 1)):
-                        link2.wait(("b", q, kind, p, o, s), buf_b[kind].at[p, q, o, h])
-                    add(block(kind, q, p, 0, o), buf_b[kind].at[p, q, o, 0], buf_b[kind].at[p, q, o, 1])
-                    if o == 2:
-                        for s, h in ((3, 0), (1, 1)):
-                            link2.send(("c", q, kind, p, s), block(kind, q, p, 0, 2, h),
-                                       buf_c[kind].at[p, q, h], to[1 - p][s])
-            for s, h in ((3, 0), (1, 1)):
-                for p in (0, 1):
-                    link2.wait(("c", q, kind, p, s), buf_c[kind].at[p, q, h])
-                    add(block(kind, q, p, 0, s, h), buf_c[kind].at[p, q, h])
-                    link2.send(("d", q, kind, p, s), block(kind, q, p, 0, s), buf_d[kind].at[p, q, h], to[1 - p][s])
+                        link2.send(("c", q, kind, p, s), block(kind, q, p, 0, 2, h),
+                                   buf_c[kind].at[p, q, h], to[1 - p][s])
+        for s, h in ((3, 0), (1, 1)):
+            for p in (0, 1):
+                link2.wait(("c", q, kind, p, s), buf_c[kind].at[p, q, h])
+                add(block(kind, q, p, 0, s, h), buf_c[kind].at[p, q, h])
+                link2.send(("d", q, kind, p, s), block(kind, q, p, 0, s), buf_d[kind].at[p, q, h], to[1 - p][s])
 
     def wait_d(q, kind):
         for p in (0, 1):
             for s, h in ((3, 0), (1, 1)):
                 link2.wait(("d", q, kind, p, s), buf_d[kind].at[p, q, h])
 
-    def r4(q):
-        for kind in kinds:
-            wait_d(q, kind)
-            for p in (0, 1):
-                add(block(kind, q, p, 0, 0), buf_d[kind].at[p, q, 0], buf_d[kind].at[p, q, 1])
-            link2.send(("e", kind), term[kind].at[zr[0], x, y], buf_e[kind], partner)
+    def r4(q, kind):
+        wait_d(q, kind)
+        for p in (0, 1):
+            add(block(kind, q, p, 0, 0), buf_d[kind].at[p, q, 0], buf_d[kind].at[p, q, 1])
+        link2.send(("e", kind), term[kind].at[zr[0], x, y], buf_e[kind], partner)
 
     for q in (0, 1):
-        for kind in kinds:
-            terms(q, kind)
-            r1(q, kind)
+        terms(q, "dn")
+        r1(q, "dn")
+
+    last(0, "dn")
+    last(1, "dn")
+
+    @pl.loop(0, 8)
+    def _(g):
+        for n in range(4):
+            cols = pl.ds(512 * n, 512)
+            wd[ds(g, 96), cols] = fdn[div(g, 4), rem(g, 4), :, :, cols].astype(F32).reshape(96, 512).astype(BF16)
+
+    r2(0, "dn")
+    dy = rows_of(rdy)
+
+    @pl.loop(0, 3)
+    def _(n):
+        gh[:, ds(n, 256)] = dot(dy, wd[ds(n, 256), :], ((1,), (1,)))
+
+    @pl.loop(0, 3)
+    def _(n):
+        cols = ds(n, 256)
+        ups = pl.ds(pl.multiple_of(FF + n * 256, 256), 256)
+        gate, up, grad = gu[:, cols], gu[:, ups], gh[:, cols]
+        sig = jax.nn.sigmoid(gate)
+        ggu[:, cols] = (grad * up * sig * (1.0 + gate * (1.0 - sig))).astype(BF16)
+        ggu[:, ups] = (grad * (gate * sig)).astype(BF16)
+
+    @pl.loop(0, 8)
+    def _(n):
+        xt[ds(n, 256), :] = rows_of(rx, ds(n, 256)).T
+
+    terms(0, "in")
+    r1(0, "in")
+    r2(1, "dn")
+    terms(1, "in")
+    r1(1, "in")
 
     def rows_back(which, src, dst):
         for number in range(1, 8):
@@ -430,10 +447,13 @@
         odx[:, :, ds(g, 256)] = value.astype(BF16).reshape(8, CAP, 256)
 
     rows_back(1, odx, bdx)
-    r2(0)
-    r2(1)
-    r3(0)
-    r4(0)
+    r2(0, "in")
+    r3(0, "dn")
+    r2(1, "in")
+    r4(0, "dn")
+    r3(0, "in")
+    r3(1, "dn")
+    r4(0, "in")
     for which, dst in enumerate((box, bdx)):
         for kind, k, zd in exchange_targets(x, y, z, c):
             if kind == 0:
@@ -456,7 +476,7 @@
         layer[:, cols] = (dot(high_t, value) + dot(low_t, value)).astype(BF16)
         gtok[:, cols] = dot(back_t, rows_of(bdx, cols)).astype(BF16)
 
-    r3(1)
+    r3(1, "in")
     for kind, out in (("dn", gdn), ("in", gin)):
         wait_d(1, kind)
         link2.wait(("e", kind), buf_e[kind])

time: 145 us -> 136 us (0.938)
  Pallas kernels: 137 us -> 128 us
    pallas_call x1, Pallas kernels: 137 us -> 128 us  [call(): pl.pallas_call(kernel, name='expert_window', out_shape=(jax.ShapeDtypeStr...]
where the time goes in v3:
time: 136 us; the launch traced here: 135 us
  Pallas kernels  128 us (94%)
  local copies, waits for them, and re-layouts  6.71 us (5%)
    pallas_call x1, Pallas kernels, call(): pl.pallas_call(kernel, name='expert_window', out_shape=(jax.ShapeDtypeStr...  128 us
    unnamed x10, local copies, waits for them, and re-layouts  4.65 us

profile of v3, /device:TPU:2, one launch (start us, length us, event | category | flops | bytes accessed | tf_op | source)
XLA Modules:
  0.0 135.3 jit_solution(2159152980812182358)
XLA Ops:
  0.6 1.6 %copy.10 = bf16[8,8,2,768]{3,1,2,0:T(8,128)(2,1)} copy(bf16[8,8,2,768]{3,2,1,0:T(2,128)(2,1)} %bitcast.8) | data formatting | bytes 393216
  2.3 128.0 %expert_window.1 = (bf16[128,2048]{1,0:T(8,128)(2,1)}, bf16[128,2048]{1,0:T(8,128)(2,1)}, f32[64,1536]{1,0:T(8,128)}, f32[24,2048]{1,0:T(8,128)}) custom-call(bf16[128,2048]{1,0:T(8,128)(2,1)} %tok_hbm.1, bf16[128,2048]{1,0:T(8,128)(2,1)} %cot_hbm.1, s32[6,128]{1,0:T(8,128)} %bitcast.11, f32[6,128]{1,0:T(8,128)} %bitcast.12, bf16[64,1536]{1,0:T(8,128)(2,1)} %bitcast.7, ...), custom_call_target="tpu_custom_call" | custom-call | tf_op jit(solution)/shard_map/expert_window/pallas_call | solution.py:498
  130.2 0.0 copy-start.1
  130.2 2.1 %reshape.14 = f32[1,64,2,768]{3,2,1,0:T(2,128)} reshape(f32[64,1536]{1,0:T(8,128)} %get-tuple-element.10) | data formatting | bytes 786432 | tf_op jit(solution)/shard_map/reshape | solution.py:557
  132.3 0.0 copy-done.1
  132.3 0.0 copy-start
  132.3 0.8 copy.14
  133.1 0.4 copy-done
  133.5 0.0 copy-start.2
  133.5 0.8 copy.15
  134.3 0.3 copy-done.2
  134.6 0.7 copy.16
Async XLA Ops:
  130.2 2.1 %copy-start.1 = (bf16[128,2048]{1,0:T(8,128)(2,1)S(1)}, bf16[128,2048]{1,0:T(8,128)(2,1)}, u32[]{:S(2)}) copy-start(bf16[128,2048]{1,0:T(8,128)(2,1)} %get-tuple-element.16) | copy-start | bytes 1572868
  132.3 1.2 copy-start
  133.5 1.1 copy-start.2

commit v4 on v3

--- a/solution.py
+++ b/solution.py
@@ -112,18 +112,20 @@
     return ref[:, :, cols].reshape(ROWS, cols.size)
 
 
-def kernel(tok_hbm, cot_hbm, rt, rw, win, wdn, layer, gtok, gin, gdn,
-           tok, cot, fin, fdn, wd, sx, sdy, rx, rdy, ox, odx, box, bdx,
+def kernel(tok_hbm, cot_hbm, rt, rw, win, wdn, layer_hbm, gtok_hbm, gin_hbm, gdn_hbm,
+           layer, gtok, gin, gdn, raw, flat, wide, tok, cot, fin, fdn, wd, sx, sdy, rx, rdy, ox, odx, box, bdx,
            back, whi, wlo, xt, gu, gh, hid, hidt, ggu,
            tin, tdn, a_in, a_dn, b_in, b_dn, c_in, c_dn, d_in, d_dn, e_in, e_dn,
-           send_sem, recv_sem, a_send, a_recv, send_sem2, recv_sem2, r_send, r_recv, local_sem):
+           send_sem, recv_sem, a_send, a_recv, send_sem2, recv_sem2, r_send, r_recv, local_sem, out_sem):
     x, y, z, c = place()
     zh = div(z, 4)
     e = lax.axis_index("ep")
+    fetch = pltpu.make_async_copy(win, raw, local_sem.at[3])
+    fetch.start()
     greet(x, y, z, c)
     link = Link(send_sem, recv_sem, N_SEM_A)
     full = {"in": fin, "dn": fdn}
-    own = {"in": win, "dn": wdn}
+    own = {"in": flat, "dn": wdn}
     zs = (zh, 1 - zh)
     to_x = {s: device(rem(x + s, 4), y, z, c) for s in (1, 3)}
     to_y = {s: device(x, rem(y + s, 4), z, c) for s in (1, 3)}
@@ -185,14 +187,22 @@
                 link.wait(("yf", q, kind, 0, o, s), slot(kind, q, o, 2, 0, h))
                 link.wait(("xf", q, kind, 1, o, s), slot(kind, q, 2, o, 1, h))
 
+    start(0, "dn")
+    loads = []
+    for n, (src, dst) in enumerate(((tok_hbm, tok), (cot_hbm, cot), (wdn, slot("dn", 0, 0, 0)))):
+        copy = pltpu.make_async_copy(src, dst, local_sem.at[n])
+        copy.start()
+        loads.append(copy)
+    fetch.wait()
+    wide[...] = raw[...].astype(F32)
+    halves = [wide[:, n, :].astype(BF16) for n in (0, 1)]
+    for n in (0, 1):
+        flat[:, FF * n:FF * (n + 1)] = halves[n]
+    for n in (0, 1):
+        fin[zh, x, y, :, FF * n:FF * (n + 1)] = halves[n]
     for kind in ("in", "dn"):
         link.send(("z", kind), own[kind], slot(kind, 0, 0, 0), partner)
     start(0, "in")
-    loads = []
-    for n, (src, dst) in enumerate(((tok_hbm, tok), (cot_hbm, cot), (wdn, slot("dn", 0, 0, 0)), (win, slot("in", 0, 0, 0)))):
-        copy = pltpu.make_async_copy(src, dst, local_sem.at[n])
-        copy.start()
-        loads.append(copy)
 
     experts = lax.broadcasted_iota(jnp.int32, (8, 128), 0)
     member = jnp.zeros((8, 128), F32)
@@ -243,7 +253,6 @@
             copy.start()
             rows.append(copy)
     third(0, "in", (1, 3))
-    start(0, "dn")
     first(1, "in")
     third(0, "in", (2,))
     link.wait(("z", "dn"), slot("dn", 1, 0, 0))
@@ -476,19 +485,64 @@
         layer[:, cols] = (dot(high_t, value) + dot(low_t, value)).astype(BF16)
         gtok[:, cols] = dot(back_t, rows_of(bdx, cols)).astype(BF16)
 
+    outs = []
+
+    def leave(src, dst):
+        copy = pltpu.make_async_copy(src, dst, out_sem.at[len(outs)])
+        copy.start()
+        outs.append(copy)
+
+    leave(layer, layer_hbm)
+    leave(gtok, gtok_hbm)
     r3(1, "in")
-    for kind, out in (("dn", gdn), ("in", gin)):
+    for kind in ("dn", "in"):
         wait_d(1, kind)
         link2.wait(("e", kind), buf_e[kind])
         for p in (0, 1):
             total = block(kind, 1, p, 0, 0)[...].astype(F32) + buf_d[kind][p, 1, 0].astype(F32)
             total = total + buf_d[kind][p, 1, 1].astype(F32)
             total = total + part(kind, buf_e[kind], p)[...].astype(F32)
-            part(kind, out, p)[...] = total
+            if kind == "dn":
+                part(kind, gdn, p)[...] = total
+            else:
+                for n in (0, 1):
+                    gin[pl.ds(32 * p, 32), n, :] = total[:, FF * n:FF * (n + 1)]
+        leave(*((gdn, gdn_hbm) if kind == "dn" else (gin, gin_hbm)))
     for copy in rows:
         copy.wait_send()
     link.drain()
     link2.drain()
+    for copy in outs:
+        copy.wait()
+
+
+def deliver(*refs):
+    sources, targets, buffers, in_sem, out_sem = refs[:4], refs[4:8], refs[8:12], refs[12], refs[13]
+    arrive = [pltpu.make_async_copy(sources[n], buffers[n], in_sem.at[n]) for n in range(4)]
+    leave = [pltpu.make_async_copy(buffers[n], targets[n], out_sem.at[n]) for n in range(4)]
+    for copy in arrive:
+        copy.start()
+    for n in range(4):
+        arrive[n].wait()
+        leave[n].start()
+    for copy in leave:
+        copy.wait()
+
+
+RESULTS = (((128, D), BF16), ((128, D), BF16), ((64, 2, FF), F32), ((24, D), F32))
+
+
+def hand_over(results):
+    anyspace = pl.BlockSpec(memory_space=pl.ANY)
+    return pl.pallas_call(
+        deliver,
+        name="deliver",
+        out_shape=tuple(jax.ShapeDtypeStruct(shape, kind) for shape, kind in RESULTS),
+        in_specs=[anyspace] * 4,
+        out_specs=[anyspace] * 4,
+        scratch_shapes=[pltpu.VMEM(shape, kind) for shape, kind in RESULTS]
+        + [pltpu.SemaphoreType.DMA((4,)), pltpu.SemaphoreType.DMA((4,))],
+    )(*results)
 
 
 def call(tokens, cotangent, routes, weights, win, wdn):
@@ -498,15 +552,13 @@
     return pl.pallas_call(
         kernel,
         name="expert_window",
-        out_shape=(
-            jax.ShapeDtypeStruct((128, D), BF16),
-            jax.ShapeDtypeStruct((128, D), BF16),
-            jax.ShapeDtypeStruct((64, 2 * FF), F32),
-            jax.ShapeDtypeStruct((24, D), F32),
-        ),
+        out_shape=tuple(jax.ShapeDtypeStruct(shape, kind) for shape, kind in RESULTS),
         in_specs=[anyspace, anyspace, vmem, vmem, anyspace, anyspace],
-        out_specs=[vmem] * 4,
-        scratch_shapes=[
+        out_specs=[anyspace] * 4,
+        scratch_shapes=[pltpu.VMEM(shape, kind) for shape, kind in RESULTS] + [
+            pltpu.VMEM((64, 2, FF), BF16),
+            pltpu.VMEM((64, 2 * FF), BF16),
+            pltpu.VMEM((64, 2, FF), F32),
             pltpu.VMEM((128, D), BF16),
             pltpu.VMEM((128, D), BF16),
             pltpu.VMEM((2, 4, 4, 64, 2 * FF), BF16),
@@ -543,6 +595,7 @@
             pltpu.SemaphoreType.DMA((16,)),
             pltpu.SemaphoreType.DMA((16,)),
             pltpu.SemaphoreType.DMA((4,)),
+            pltpu.SemaphoreType.DMA((4,)),
         ],
         compiler_params=pltpu.CompilerParams(
             collective_id=0, has_side_effects=True, vmem_limit_bytes=60 * 1024 * 1024
@@ -551,9 +604,9 @@
 
 
 def local(tokens, routes, route_weight, w_in, w_down, cotangent):
-    layer_out, grad_tokens, grad_in, grad_down = call(
-        tokens, cotangent, routes.T, route_weight.T, w_in[0].reshape(64, 2 * FF), w_down[0]
-    )
+    layer_out, grad_tokens, grad_in, grad_down = hand_over(call(
+        tokens, cotangent, routes.T, route_weight.T, w_in[0], w_down[0]
+    ))
     return layer_out, grad_tokens, grad_in.reshape(w_in.shape), grad_down.reshape(w_down.shape)
 
 

time: 136 us -> 131 us (0.963)
  local copies, waits for them, and re-layouts: 6.71 us -> 0 us
    unnamed x10 -> x0, local copies, waits for them, and re-layouts: 4.65 us -> none
    reshape x1 -> x0, local copies, waits for them, and re-layouts: 2.06 us -> none  [local(): grad_in.reshape(w_in.shape)]
    pallas_call x1 -> x2, Pallas kernels: 128 us -> 129 us  [the longest x1 127 us: call(): pl.pallas_call(kernel, name='expert_window', out_shape=tuple((jax.ShapeDt...]
where the time goes in v4:
time: 131 us; the launch traced here: 130 us
  Pallas kernels  129 us (98%)
    pallas_call x1, Pallas kernels, call(): pl.pallas_call(kernel, name='expert_window', out_shape=tuple((jax.ShapeDt...  127 us

profile of v4, /device:TPU:2, one launch (start us, length us, event | category | flops | bytes accessed | tf_op | source)
XLA Modules:
  0.0 130.0 jit_solution(2812661294157440878)
XLA Ops:
  0.6 127.1 %expert_window.1 = (bf16[128,2048]{1,0:T(8,128)(2,1)}, bf16[128,2048]{1,0:T(8,128)(2,1)}, f32[64,2,768]{2,1,0:T(2,128)}, f32[24,2048]{1,0:T(8,128)}) custom-call(bf16[128,2048]{1,0:T(8,128)(2,1)} %tok_hbm.1, bf16[128,2048]{1,0:T(8,128)(2,1)} %cot_hbm.1, s32[6,128]{1,0:T(8,128)} %bitcast.8, f32[6,128]{1,0:T(8,128)} %bitcast.9, bf16[64,2,768]{2,1,0:T(2,128)(2,1)} %bitcast.6, ...), custom_call_target="tpu_custom_call" | custom-call | tf_op jit(solution)/shard_map/expert_window/pallas_call | solution.py:552
  127.8 2.3 %deliver.1 = (bf16[128,2048]{1,0:T(8,128)(2,1)}, bf16[128,2048]{1,0:T(8,128)(2,1)}, f32[64,2,768]{2,1,0:T(2,128)}, f32[24,2048]{1,0:T(8,128)}) custom-call(bf16[128,2048]{1,0:T(8,128)(2,1)} %get-tuple-element.12.refs_0_, bf16[128,2048]{1,0:T(8,128)(2,1)} %get-tuple-element.13.refs_1_, f32[64,2,768]{2,1,0:T(2,128)} %get-tuple-element.14.refs_2_, ...), custom_call_target="tpu_custom_call" | custom-call | tf_op jit(solution)/shard_map/deliver/pallas_call | solution.py:537

commit v5 on v4

--- a/solution.py
+++ b/solution.py
@@ -232,10 +232,8 @@
     rx[c] = sx[mine]
     rdy[c] = sdy[mine]
 
+    first(0, "dn")
     first(0, "in")
-    second(0, "in")
-    link.wait(("z", "in"), slot("in", 1, 0, 0))
-    start(1, "in")
     rows = []
     for which, (src, dst) in enumerate(((sx, rx), (sdy, rdy))):
         for kind, k, zd in exchange_targets(x, y, z, c):
@@ -252,13 +250,15 @@
             )
             copy.start()
             rows.append(copy)
+    second(0, "in")
     third(0, "in", (1, 3))
+    link.wait(("z", "in"), slot("in", 1, 0, 0))
+    start(1, "in")
+    third(0, "in", (2,))
     first(1, "in")
-    third(0, "in", (2,))
     link.wait(("z", "dn"), slot("dn", 1, 0, 0))
     start(1, "dn")
     second(1, "in")
-    first(0, "dn")
     third(1, "in", (1, 3))
     first(1, "dn")
     second(0, "dn")
@@ -349,8 +349,8 @@
                     link2.send(("a", q, kind, p, o, s), block(kind, q, p, 2, o, h),
                                buf_a[kind].at[p, q, o, h], to[p][s])
 
-    def r2(q, kind):
-        for o in offsets:
+    def r2(q, kind, some=offsets):
+        for o in some:
             for p in (0, 1):
                 for s, h in ((3, 0), (1, 1)):
                     link2.wait(("a", q, kind, p, o, s), buf_a[kind].at[p, q, o, h])
@@ -368,6 +368,8 @@
                     for s, h in ((3, 0), (1, 1)):
                         link2.send(("c", q, kind, p, s), block(kind, q, p, 0, 2, h),
                                    buf_c[kind].at[p, q, h], to[1 - p][s])
+
+    def pass_on(q, kind):
         for s, h in ((3, 0), (1, 1)):
             for p in (0, 1):
                 link2.wait(("c", q, kind, p, s), buf_c[kind].at[p, q, h])
@@ -458,11 +460,17 @@
     rows_back(1, odx, bdx)
     r2(0, "in")
     r3(0, "dn")
-    r2(1, "in")
+    r2(1, "in", (2,))
+    pass_on(0, "dn")
+    r3(0, "in")
+    r2(1, "in", (1,))
     r4(0, "dn")
-    r3(0, "in")
+    pass_on(0, "in")
+    r2(1, "in", (3,))
     r3(1, "dn")
+    r2(1, "in", (0,))
     r4(0, "in")
+    pass_on(1, "dn")
     for which, dst in enumerate((box, bdx)):
         for kind, k, zd in exchange_targets(x, y, z, c):
             if kind == 0:
@@ -495,6 +503,7 @@
     leave(layer, layer_hbm)
     leave(gtok, gtok_hbm)
     r3(1, "in")
+    pass_on(1, "in")
     for kind in ("dn", "in"):
         wait_d(1, kind)
         link2.wait(("e", kind), buf_e[kind])

time: 131 us -> 127 us (0.969)
  Pallas kernels: 129 us -> 126 us
    pallas_call x1, Pallas kernels: 127 us -> 124 us  [call(): pl.pallas_call(kernel, name='expert_window', out_shape=tuple((jax.ShapeDt...]
where the time goes in v5:
time: 127 us
  Pallas kernels  126 us (99%)
    pallas_call x1, Pallas kernels, call(): pl.pallas_call(kernel, name='expert_window', out_shape=tuple((jax.ShapeDt...  124 us

profile of v5, /device:TPU:2, one launch (start us, length us, event | category | flops | bytes accessed | tf_op | source)
XLA Modules:
  0.0 127.1 jit_solution(10219179174689886365)
XLA Ops:
  0.6 124.2 %expert_window.1 = (bf16[128,2048]{1,0:T(8,128)(2,1)}, bf16[128,2048]{1,0:T(8,128)(2,1)}, f32[64,2,768]{2,1,0:T(2,128)}, f32[24,2048]{1,0:T(8,128)}) custom-call(bf16[128,2048]{1,0:T(8,128)(2,1)} %tok_hbm.1, bf16[128,2048]{1,0:T(8,128)(2,1)} %cot_hbm.1, s32[6,128]{1,0:T(8,128)} %bitcast.8, f32[6,128]{1,0:T(8,128)} %bitcast.9, bf16[64,2,768]{2,1,0:T(2,128)(2,1)} %bitcast.6, ...), custom_call_target="tpu_custom_call" | custom-call | tf_op jit(solution)/shard_map/expert_window/pallas_call | solution.py:561
  124.8 2.3 %deliver.1 = (bf16[128,2048]{1,0:T(8,128)(2,1)}, bf16[128,2048]{1,0:T(8,128)(2,1)}, f32[64,2,768]{2,1,0:T(2,128)}, f32[24,2048]{1,0:T(8,128)}) custom-call(bf16[128,2048]{1,0:T(8,128)(2,1)} %get-tuple-element.12.refs_0_, bf16[128,2048]{1,0:T(8,128)(2,1)} %get-tuple-element.13.refs_1_, f32[64,2,768]{2,1,0:T(2,128)} %get-tuple-element.14.refs_2_, ...), custom_call_target="tpu_custom_call" | custom-call | tf_op jit(solution)/shard_map/deliver/pallas_call | solution.py:546
